TPU v7x, 256 devices: a whole 4x4x8 slice. The times are simulated.
256 devices in a mesh: dp: 4 (over x), expert: 64 (over z, y, core).
Axes of the slice: x: 4, y: 4, z: 8, core: 2. Of those that a mesh axis runs over, the one named last changes fastest.
Arguments:
- queries: bfloat16 [16384, 2048], P('expert', 'dp'), may hold values from -160 to 160
- kv_pool: bfloat16 [2, 1024, 64, 2048], P(None, 'expert', None, 'dp'), may hold values from -6 to 6
- page_table: int32 [256, 4], P('expert'), may hold values from 0 to 1023, as said below
- ctx_lens: int32 [16384], P('expert'), may hold values from 2 to 256, as said below
- w_out: bfloat16 [2048, 2048], P('dp', 'expert'), may hold values from -0.59765625 to 0.59765625
- residual: bfloat16 [16384, 2048], P(('expert', 'dp')), may hold values from -3 to 3
- moe_gain: float32 [2048], replicated, may hold values from 0.25 to 1.75
- expert_ids: int32 [16384, 6], P(('expert', 'dp')), may hold values from 0 to 63, all different within a row; in each aligned block of 64 rows (0 to 63, 64 to 127, ...) at most 12 rows name the same one
- route_weights: float32 [16384, 6], P(('expert', 'dp')), may hold values from 0.05 to 0.4
- w_gate: bfloat16 [64, 2048, 1408], P('expert', 'dp'), may hold values from -0.125 to 0.125
- w_up: bfloat16 [64, 2048, 1408], P('expert', 'dp'), may hold values from -0.125 to 0.125
- w_down: bfloat16 [64, 1408, 2048], P('expert', 'dp'), may hold values from -0.15625 to 0.15625
- final_gain: float32 [2048], replicated, may hold values from 0.25 to 1.75
Outputs:
- layer_out: bfloat16 [16384, 2048], P(('expert', 'dp'))
Inputs may be any that keep to these rules, and one draw needn't show every extreme that they name: `page_table`: the 4 pages of sequence s are distinct pages of group s // 4, which owns pages g * 16 to g * 16 + 15; every page belongs to exactly one sequence. `ctx_lens`: the first row of every sequence reads all 256 positions. `expert_ids`: each row names 6 distinct experts; among the 64 rows of one device (aligned blocks of 64 rows) no expert is named more than 12 times.
All inputs are finite; a program needn't handle non-finite values.
Results may differ from a plain program's by a relative error of at most 0.017.
Values may be sent and summed in bfloat16 or wider, within the bound.
A program may use at most 128 MiB of HBM per device.

v0:
```python
import math

import jax
import jax.numpy as jnp
from jax import lax
from jax.sharding import PartitionSpec as P

HD = 128
TOP = 6
CTX = 256


def normalize(values, gain):
    mean_sq = jnp.mean(values * values, axis=-1, keepdims=True)
    return values * lax.rsqrt(mean_sq + 1e-06) * gain


def fetch_experts(w_gate, w_up, w_down):
    return (
        lax.all_gather(w_gate, "dp", axis=1, tiled=True),
        lax.all_gather(w_up, "dp", axis=1, tiled=True),
        lax.all_gather(w_down, "dp", axis=1, tiled=True),
    )


def shards(
    queries,
    kv_pool,
    page_table,
    ctx_lens,
    w_out,
    residual,
    moe_gain,
    expert_ids,
    route_weights,
    w_gate,
    w_up,
    w_down,
    final_gain,
):
    replicas = None
    scale = 1.0 / math.sqrt(HD)
    group_rows = queries.shape[0]
    local_feats = queries.shape[1]
    local_heads = local_feats // HD
    seq_count = page_table.shape[0]
    seq_rows = group_rows // seq_count
    pool_here = kv_pool.shape[1]
    local_pages = page_table - lax.axis_index("expert") * pool_here
    keys = kv_pool[0][local_pages].reshape(seq_count, CTX, local_heads, HD)
    values = kv_pool[1][local_pages].reshape(seq_count, CTX, local_heads, HD)
    asked = queries.reshape(seq_count, seq_rows, local_heads, HD)
    scores = jnp.einsum("sqhd,skhd->shqk", asked, keys, preferred_element_type=jnp.float32) * scale
    lengths = ctx_lens.reshape(seq_count, seq_rows)
    visible = (jnp.arange(CTX, dtype=jnp.int32)[None, None, :] < lengths[:, :, None])[:, None]
    scores = jnp.where(visible, scores, -1e30)
    top_score = jnp.max(scores, axis=-1, keepdims=True)
    expo = jnp.where(visible, jnp.exp(scores - top_score), 0.0)
    probs = (expo / jnp.sum(expo, axis=-1, keepdims=True)).astype(jnp.bfloat16)
    mixed = jnp.einsum("shqk,skhd->sqhd", probs, values, preferred_element_type=jnp.float32)
    context = mixed.astype(jnp.bfloat16).reshape(group_rows, local_feats)
    columns = lax.all_gather(w_out, "expert", axis=1, tiled=True)
    projected = lax.psum_scatter(
        jnp.dot(context, columns, preferred_element_type=jnp.float32).astype(jnp.bfloat16),
        "dp",
        scatter_dimension=0,
        tiled=True,
    ).astype(jnp.float32)
    hidden_state = residual.astype(jnp.float32) + projected
    moe_input = normalize(hidden_state, moe_gain).astype(jnp.bfloat16)
    rows_here = moe_input.shape[0]
    experts = lax.axis_size("expert")
    slots = max(2, min(rows_here, 2 * rows_here * TOP // experts))
    flat_ids = expert_ids.reshape(-1)
    marks = (flat_ids[:, None] == jnp.arange(experts, dtype=jnp.int32)[None, :]).astype(jnp.int32)
    before = jnp.sum((jnp.cumsum(marks, axis=0) - 1) * marks, axis=1)
    target = (flat_ids * slots + before).reshape(rows_here, TOP)
    placing = jnp.any(
        jnp.arange(experts * slots, dtype=jnp.int32)[:, None, None] == target[None], axis=-1
    )
    outbound = jnp.dot(placing.astype(jnp.bfloat16), moe_input, preferred_element_type=jnp.float32)
    outbound = outbound.astype(jnp.bfloat16).reshape(experts, slots, moe_input.shape[1])
    replicas = fetch_experts(w_gate, w_up, w_down)
    gate_full, up_full, down_full = replicas
    arrived = lax.all_to_all(outbound, "expert", split_axis=0, concat_axis=0, tiled=True)
    flat = arrived.reshape(-1, arrived.shape[2])
    gate = jnp.dot(flat, gate_full[0], preferred_element_type=jnp.float32)
    up_part = jnp.dot(flat, up_full[0], preferred_element_type=jnp.float32)
    expert_mid = (jax.nn.silu(gate) * up_part).astype(jnp.bfloat16)
    done = jnp.dot(expert_mid, down_full[0], preferred_element_type=jnp.float32).astype(
        jnp.bfloat16
    )
    done = done.reshape(arrived.shape[0], arrived.shape[1], arrived.shape[2])
    returned = lax.all_to_all(done, "expert", split_axis=0, concat_axis=0, tiled=True)
    answers = returned.reshape(experts * slots, returned.shape[2])[target]
    moe = jnp.sum(route_weights[:, :, None] * answers.astype(jnp.float32), axis=1)
    combined = hidden_state + moe
    return normalize(combined, final_gain).astype(jnp.bfloat16)


def solution(mesh):
    return jax.shard_map(
        shards,
        mesh=mesh,
        in_specs=(
            P("expert", "dp"),
            P(None, "expert", None, "dp"),
            P("expert", None),
            P("expert"),
            P("dp", "expert"),
            P(("expert", "dp"), None),
            P(),
            P(("expert", "dp"), None),
            P(("expert", "dp"), None),
            P("expert", "dp", None),
            P("expert", "dp", None),
            P("expert", "dp", None),
            P(),
        ),
        out_specs=P(("expert", "dp"), None),
        check_vma=False,
    )
```

profile of v0, /device:TPU:1, one launch (start us, length us, event | category | flops | bytes accessed | tf_op | source)
XLA Modules:
  0.0 469.0 jit_solution(8235177650475701003)
XLA Ops:
  8.1 1.7 slice_bitcast_fusion
  12.7 1.6 fusion.34
  14.3 1.6 fusion.18
  16.1 75.6 %all-gather.5.cloned.1.call-done = bf16[512,2048]{0,1:T(8,128)(2,1)} async-done(((bf16[512,32]{0,1:T(8,128)(2,1)}), bf16[512,2048]{0,1:T(8,128)(2,1)}) %all-gather.5.cloned.1.call-update) | async-done | bytes 2097168 | tf_op jit(solution)/shard_map/all_gather | solution.py:62
  91.7 3.4 convolution_convert_fusion.1
  97.4 0.9 reduce-window.6
  99.2 18.0 %reduce-scatter.2.cloned.1.call-done = bf16[64,2048]{1,0:T(8,128)(2,1)} async-done(((bf16[256,2048]{1,0:T(8,128)(2,1)}), bf16[64,2048]{1,0:T(8,128)(2,1)}) %reduce-scatter.2.cloned.1.call-update) | async-done | bytes 262160 | tf_op jit(solution)/shard_map/reduce_scatter | solution.py:63
  117.1 1.1 multiply_reduce_fusion.2
  118.3 2.0 convolution_convert_fusion
  120.3 2.7 reshape.82
  123.0 106.8 %all_to_all.10 = bf16[64,12,2048]{2,1,0:T(8,128)(2,1)} all-to-all(bf16[64,12,2048]{2,1,0:T(8,128)(2,1)} %reshape.82), channel_id=1, replica_groups=mesh['dp'=4,'expert'=64] {'expert'}, dimensions={0} | all-to-all | bytes 6291456 | tf_op jit(solution)/shard_map/all_to_all | solution.py:85
  229.8 4.7 %reshape.83 = bf16[768,2048]{1,0:T(8,128)(2,1)S(1)} reshape(bf16[64,12,2048]{2,1,0:T(8,128)(2,1)} %all_to_all.10) | data formatting | bytes 6291456 | tf_op jit(solution)/shard_map/reshape | solution.py:86
  234.5 9.3 %fusion.3 = f32[768,1408]{1,0:T(8,128)} fusion(bf16[768,2048]{1,0:T(8,128)(2,1)S(1)} %reshape.83, bf16[1,2048,1408]{2,1,0:T(8,128)(2,1)} %all-gather.9.cloned.1.call-done), kind=kOutput, calls=%fused_computation.6 | convolution fusion | flops 4429185024 | bytes 13238272 | tf_op jit(solution)/shard_map/dot_general | solution.py:88
  243.8 6.6 %all-gather.11.cloned.1.call-done = bf16[1,1408,2048]{2,1,0:T(8,128)(2,1)} async-done(((bf16[1,352,2048]{2,1,0:T(8,128)(2,1)}), bf16[1,1408,2048]{2,1,0:T(8,128)(2,1)}) %all-gather.11.cloned.1.call-update) | async-done | bytes 5767184 | tf_op jit(solution)/shard_map/all_gather | solution.py:22
  250.4 66.3 %all-gather.7.cloned.1.call-done = bf16[1,2048,1408]{2,1,0:T(8,128)(2,1)} async-done(((bf16[1,512,1408]{2,1,0:T(8,128)(2,1)}), bf16[1,2048,1408]{2,1,0:T(8,128)(2,1)}) %all-gather.7.cloned.1.call-update) | async-done | bytes 5767184 | tf_op jit(solution)/shard_map/all_gather | solution.py:20
  316.8 17.6 %fusion.9 = bf16[768,2048]{1,0:T(8,128)(2,1)} fusion(bf16[1,1408,2048]{2,1,0:T(8,128)(2,1)} %all-gather.11.cloned.1.call-done, f32[768,1408]{1,0:T(8,128)} %fusion.3, bf16[768,2048]{1,0:T(8,128)(2,1)S(1)} %reshape.83, bf16[1,2048,1408]{2,1,0:T(8,128)(2,1)} %all-gather.7.cloned.1.call-done), kind=kOutput, calls=%fused_computation.13 | convolution fusion | flops 8866430976 | bytes 22151168 | tf_op jit(solution)/shard_map/dot_general | solution.py:90
  334.3 6.1 %reshape.84 = bf16[64,12,2048]{2,1,0:T(8,128)(2,1)} reshape(bf16[768,2048]{1,0:T(8,128)(2,1)} %fusion.9) | data formatting | bytes 6291456 | tf_op jit(solution)/shard_map/reshape | solution.py:93
  340.4 11.1 %all-to-all-start.1 = ((bf16[64,12,2048]{2,1,0:T(8,128)(2,1)}), bf16[64,12,2048]{2,1,0:T(8,128)(2,1)}, u32[]{:S(2)}, u32[]{:S(2)}) async-start(bf16[64,12,2048]{2,1,0:T(8,128)(2,1)} %reshape.84), calls=%async_computation.2 | async-start | bytes 8388608 | tf_op jit(solution)/shard_map/all_to_all | solution.py:94
  351.8 94.0 %all-to-all-done.1 = bf16[64,12,2048]{2,1,0:T(8,128)(2,1)} async-done(((bf16[64,12,2048]{2,1,0:T(8,128)(2,1)}), bf16[64,12,2048]{2,1,0:T(8,128)(2,1)}, u32[]{:S(2)}, u32[]{:S(2)}) %all-to-all-start.1) | async-done | bytes 3145760 | tf_op jit(solution)/shard_map/all_to_all | solution.py:94
  445.9 4.7 %reshape.85 = bf16[768,2048]{1,0:T(8,128)(2,1)S(1)} reshape(bf16[64,12,2048]{2,1,0:T(8,128)(2,1)} %all-to-all-done.1) | data formatting | bytes 6291456 | tf_op jit(solution)/shard_map/reshape | solution.py:95
  450.6 3.1 gather_fusion.2
  453.7 3.9 reshape.118
  457.7 3.7 multiply_reduce_fusion
  461.7 0.8 multiply_convert_fusion.1
  (58 shorter events, 8.2 us)
Async XLA Ops:
  6.5 85.1 %all-gather.5.cloned.1.call-start = ((), (), s32[]{:S(2)}) async-start(), calls=%async_computation.3 | async-start | bytes 2129920 | tf_op jit(solution)/shard_map/all_gather | solution.py:62
  7.3 109.9 %reduce-scatter.2.cloned.1.call-start = ((), (), s32[]{:S(2)}) async-start(), calls=%async_computation.4 | async-start | bytes 1310720 | tf_op jit(solution)/shard_map/reduce_scatter | solution.py:63
  8.1 2.7 copy-start.2
  8.1 3.5 copy-start.8
  11.6 1.1 copy-start.3
  91.7 5.3 %copy-start.4 = (s32[64,6]{0,1:T(8,128)S(1)}, s32[64,6]{0,1:T(8,128)}, u32[]{:S(2)}) copy-start(s32[64,6]{0,1:T(8,128)} %param.20) | copy-start | bytes 4612
  91.7 25.5 %copy-start = (bf16[64,2048]{1,0:T(8,128)(2,1)S(1)}, bf16[64,2048]{1,0:T(8,128)(2,1)}, u32[]{:S(2)}) copy-start(bf16[64,2048]{1,0:T(8,128)(2,1)} %param.18) | copy-start | bytes 786436
  91.7 26.6 %copy-start.5 = (f32[2048]{0:T(1024)S(1)}, f32[2048]{0:T(1024)}, u32[]{:S(2)}) copy-start(f32[2048]{0:T(1024)} %param.19) | copy-start | bytes 24580
  95.1 139.5 %all-gather.9.cloned.1.call-start = ((), (), s32[]{:S(2)}) async-start(), calls=%async_computation.6 | async-start | bytes 7208960 | tf_op jit(solution)/shard_map/all_gather | solution.py:21
  95.8 154.6 %all-gather.11.cloned.1.call-start = ((), (), s32[]{:S(2)}) async-start(), calls=%async_computation.7 | async-start | bytes 7208960 | tf_op jit(solution)/shard_map/all_gather | solution.py:22
  96.4 220.4 %all-gather.7.cloned.1.call-start = ((), (), s32[]{:S(2)}) async-start(), calls=%async_computation.5 | async-start | bytes 7208960 | tf_op jit(solution)/shard_map/all_gather | solution.py:20
  340.4 11.3 %copy-start.7 = (f32[64,6]{0,1:T(8,128)S(1)}, f32[64,6]{0,1:T(8,128)}, u32[]{:S(2)}) copy-start(f32[64,6]{0,1:T(8,128)} %param.21) | copy-start | bytes 4612
  340.4 105.5 %all-to-all-start.1 = ((bf16[64,12,2048]{2,1,0:T(8,128)(2,1)}), bf16[64,12,2048]{2,1,0:T(8,128)(2,1)}, u32[]{:S(2)}, u32[]{:S(2)}) async-start(bf16[64,12,2048]{2,1,0:T(8,128)(2,1)} %reshape.84), calls=%async_computation.2 | async-start | bytes 8388608 | tf_op jit(solution)/shard_map/all_to_all | solution.py:94
  453.7 7.7 %copy-start.1 = (bf16[64,2048]{1,0:T(8,128)(2,1)S(1)}, bf16[64,2048]{1,0:T(8,128)(2,1)}, u32[]{:S(2)}) copy-start(bf16[64,2048]{1,0:T(8,128)(2,1)} %reduce-scatter.2.cloned.1.call-done) | copy-start | bytes 786436
  457.7 4.0 copy-start.6
Sparse Core Ops, SparseCore 0:
  10.1 81.5 all-gather.4
  95.2 21.8 reduce-scatter.1
  119.1 64.9 all-gather.8
  185.9 64.4 all-gather.10
  252.2 64.4 all-gather.6
where the time goes:
time: 471 us; the launch traced here: 469 us
  waiting for transfers between devices  263 us (56%)
  blocking collectives  107 us (23%)
  matrix products  35.4 us (8%)
  local copies, waits for them, and re-layouts  31.1 us (7%)
  between operations  13.4 us (3%)
  starting transfers between devices  11.2 us (2%)
  other arithmetic  8.07 us (2%)
    all_to_all x1, blocking collectives, shards(): lax.all_to_all(outbound, 'expert', split_axis=0, concat_axis=0, tiled=True)  107 us
    all_to_all x1, waiting for transfers between devices, shards(): lax.all_to_all(done, 'expert', split_axis=0, concat_axis=0, tiled=True)  94 us
    all_gather x1, waiting for transfers between devices, shards(): columns = lax.all_gather(w_out, 'expert', axis=1, tiled=True)  75.6 us
    all_gather x1, waiting for transfers between devices, fetch_experts(): lax.all_gather(w_gate, 'dp', axis=1, tiled=True)  66.3 us
    reduce_scatter x1, waiting for transfers between devices, shards(): lax.psum_scatter(jnp.dot(context, columns, preferred_element_type=jnp.flo...  18 us
    dot_general x1, matrix products, shards(): jnp.dot(expert_mid, down_full[0], preferred_element_type=jnp.float32)  17.6 us
    all_to_all x1, starting transfers between devices, shards(): lax.all_to_all(done, 'expert', split_axis=0, concat_axis=0, tiled=True)  11.1 us
  transfers between devices with their start and end apart: 6, of which 5 were waited for; matrix products, arithmetic and copies ran while one was open for 7% of the time, Pallas kernels for 0%

commit v1 on v0

v1 whole, which is shorter than its diff:
```python
import functools
import math

import jax
import jax.numpy as jnp
from jax import lax
from jax.experimental import pallas as pl
from jax.experimental.pallas import tpu as pltpu
from jax.sharding import PartitionSpec as P

HD = 128
TOP = 6
CTX = 256
CAP = 12
NP = 8
CHUNKS = 4
MESH = pl.DeviceIdType.MESH
F32 = jnp.float32
BF16 = jnp.bfloat16


def normalize(values, gain):
    mean_sq = jnp.mean(values * values, axis=-1, keepdims=True)
    return values * lax.rsqrt(mean_sq + 1e-06) * gain


def iota(shape, axis):
    return lax.broadcasted_iota(jnp.int32, shape, axis)


def dot(a, b):
    return jnp.dot(a, b, preferred_element_type=F32)


def moe_kernel(
    sizes,
    x_ref,
    hid_ref,
    ids_ref,
    rw_ref,
    wg_ref,
    wu_ref,
    wd_ref,
    gain_ref,
    out_ref,
    wgf,
    wuf,
    wdf,
    rows,
    route_out,
    route,
    snd,
    xin,
    mid,
    yout,
    ans,
    wcomb,
    psnd,
    prcv,
    comb,
    loc_sem,
    gu_s,
    gu_r,
    wd_s,
    wd_r,
    za_s,
    za_r,
    ya_s,
    ya_r,
    ry_s,
    ry_r,
    rz_s,
    rz_r,
):
    nd, nz, order = sizes
    pos = {off: i for i, off in enumerate(order)}
    groups = 2
    per = nz // groups
    d = lax.axis_index("dp")
    e = lax.axis_index("expert")
    z = e // NP
    p = lax.rem(e, NP)
    n_rows, width = x_ref.shape
    kd = wg_ref.shape[0]
    ff = wg_ref.shape[1]
    kf = wd_ref.shape[0]
    cw = width // CHUNKS
    seg = per * CAP
    gsz = NP * seg
    right = lax.rem(d + 1, nd)
    left = lax.rem(d + nd - 1, nd)
    sends = []

    def plane(j):
        return (d, z * NP + lax.rem(p + j, NP))

    def line(off):
        return (d, lax.rem(z + off, nz) * NP + p)

    def remote(src, dst, s, r, to):
        c = pltpu.make_async_remote_copy(
            src_ref=src, dst_ref=dst, send_sem=s, recv_sem=r, device_id=to, device_id_type=MESH
        )
        c.start()
        sends.append(c)
        return c

    barrier = pltpu.get_barrier_semaphore()
    peers = [(right, e), (left, e)] + [line(o) for o in range(1, nz)] + [plane(j) for j in range(1, NP)]
    for peer in peers:
        pl.semaphore_signal(barrier, inc=1, device_id=peer, device_id_type=MESH)
    pl.semaphore_wait(barrier, len(peers))

    rows[pl.ds(0, n_rows), :] = x_ref[...]
    lanes = ids_ref.shape[1]
    experts = nz * NP
    named = jnp.zeros((experts, lanes), F32)
    share = jnp.zeros((experts, lanes), F32)
    for k in range(TOP):
        hit = ids_ref[k : k + 1, :] == iota((experts, lanes), 0)
        named = named + jnp.where(hit, 1.0, 0.0)
        share = share + jnp.where(hit, rw_ref[k : k + 1, :], 0.0)
    upper = jnp.where(iota((lanes, lanes), 0) < iota((lanes, lanes), 1), 1.0, 0.0).astype(BF16)
    rank = dot(named.astype(BF16), upper)
    rank = jnp.where(named > 0.5, rank, -1.0)
    for i in range(nz):
        route_out[i, 0:NP, :] = rank[i * NP : (i + 1) * NP, :]
        route_out[i, NP : 2 * NP, :] = share[i * NP : (i + 1) * NP, :]
    own_route = pltpu.make_async_copy(route_out.at[z], route.at[0], loc_sem.at[3])
    own_route.start()
    za = {}
    for off in order[1:]:
        slot = pos[nz - off]
        zt = lax.rem(z + off, nz)
        a = remote(route_out.at[zt], route.at[slot], za_s.at[0, off], za_r.at[0, slot], line(off))
        b = remote(
            x_ref, rows.at[pl.ds(slot * n_rows, n_rows), :], za_s.at[1, off], za_r.at[1, slot], line(off)
        )
        za[slot] = (a, b)

    gu = [(wg_ref, wgf), (wu_ref, wuf)]
    half = kd // 2
    local = []
    for m, (src, dst) in enumerate(gu):
        c = pltpu.make_async_copy(src, dst.at[pl.ds(d * kd, kd), :], loc_sem.at[m])
        c.start()
        local.append(c)
    c = pltpu.make_async_copy(wd_ref, wdf.at[pl.ds(d * kf, kf), :], loc_sem.at[2])
    c.start()
    local.append(c)
    gu_c = {}
    for m, (src, dst) in enumerate(gu):
        for side, to in ((0, right), (1, left)):
            for h in (side, 1 - side):
                gu_c[m, side, h] = remote(
                    src.at[pl.ds(h * half, half), :],
                    dst.at[pl.ds(d * kd + h * half, half), :],
                    gu_s.at[m, side, h],
                    gu_r.at[m, side, h],
                    (to, e),
                )

    slot_i = iota((gsz, per * n_rows), 0)
    expand = jnp.where(iota((gsz, NP), 0) // seg == iota((gsz, NP), 1), 1.0, 0.0).astype(BF16)
    want = lax.rem(slot_i, CAP).astype(F32)
    block_ok = lax.rem(slot_i, seg) // CAP == iota((gsz, per * n_rows), 1) // n_rows
    ya = {}

    def dispatch(g):
        for i in range(g * per, (g + 1) * per):
            if i == 0:
                own_route.wait()
            else:
                za[i][0].wait_recv()
                za[i][1].wait_recv()
        ranks = jnp.concatenate(
            [route[i, 0:NP, 0:n_rows] for i in range(g * per, (g + 1) * per)], axis=1
        )
        shares = jnp.concatenate(
            [route[i, NP : 2 * NP, 0:n_rows] for i in range(g * per, (g + 1) * per)], axis=1
        )
        pick = jnp.logical_and(dot(expand, ranks.astype(BF16)) == want, block_ok)
        pick_b = jnp.where(pick, 1.0, 0.0).astype(BF16)
        base = g * per * n_rows

        def tile(i, carry):
            cols = pl.ds(pl.multiple_of(i * 512, 512), 512)
            snd[g, :, cols] = dot(pick_b, rows[pl.ds(base, per * n_rows), cols]).astype(BF16)
            return carry

        lax.fori_loop(0, width // 512, tile, 0)
        for j in range(1, NP):
            t = lax.rem(p + j, NP)
            ya[g, j] = remote(
                snd.at[g, pl.ds(t * seg, seg), :],
                xin.at[g, pl.ds(p * seg, seg), :],
                ya_s.at[g, j],
                ya_r.at[g, j],
                plane(j),
            )
        mine = pltpu.make_async_copy(
            snd.at[g, pl.ds(p * seg, seg), :], xin.at[g, pl.ds(p * seg, seg), :], ya_s.at[g, 0]
        )
        mine.start()
        ya[g, 0] = mine
        hi = shares.astype(BF16)
        lo = (shares - hi.astype(F32)).astype(BF16)
        for part, val in ((0, hi), (1, lo)):
            full = jnp.where(pick, dot(expand, val), 0.0)
            wcomb[g, part] = jnp.transpose(full).astype(BF16)

    for g in range(groups):
        dispatch(g)

    gu_f = {}
    for m, (_, dst) in enumerate(gu):
        for side, frm, to in ((0, left, right), (1, right, left)):
            gu_c[m, side, side].wait_recv()
            at = pl.ds(frm * kd + side * half, half)
            gu_f[m, side] = remote(
                dst.at[at, :], dst.at[at, :], gu_s.at[m, side, 2], gu_r.at[m, side, 2], (to, e)
            )
    hf = kf // 2
    wd_c = {}
    for n in range(CHUNKS):
        cols = pl.ds(n * cw, cw)
        for side, to in ((0, right), (1, left)):
            for h in (side, 1 - side):
                wd_c[n, side, h] = remote(
                    wd_ref.at[pl.ds(h * hf, hf), cols],
                    wdf.at[pl.ds(d * kf + h * hf, hf), cols],
                    wd_s.at[n, side, h],
                    wd_r.at[n, side, h],
                    (to, e),
                )
    for m in range(2):
        local[m].wait()
        for side in range(2):
            gu_c[m, side, 1 - side].wait_recv()
            gu_f[m, side].wait_recv()
    wd_f = {}
    for n in range(CHUNKS):
        cols = pl.ds(n * cw, cw)
        for side, frm, to in ((0, left, right), (1, right, left)):
            wd_c[n, side, side].wait_recv()
            at = pl.ds(frm * kf + side * hf, hf)
            wd_f[n, side] = remote(
                wdf.at[at, cols], wdf.at[at, cols], wd_s.at[n, side, 2], wd_r.at[n, side, 2], (to, e)
            )

    def up_tile(g, cols):
        xs = xin[g]
        gate = dot(xs, wgf[:, cols])
        up = dot(xs, wuf[:, cols])
        mid[g, :, cols] = (gate / (1.0 + jnp.exp(-gate)) * up).astype(BF16)

    full_tiles = ff // 256
    for g in range(groups):
        for j in range(1, NP):
            ya[g, j].wait_recv()
        ya[g, 0].wait()

        def step(i, carry, g=g):
            up_tile(g, pl.ds(pl.multiple_of(i * 256, 256), 256))
            return carry

        lax.fori_loop(0, full_tiles, step, 0)
        if ff % 256:
            up_tile(g, pl.ds(full_tiles * 256, ff % 256))

    ry = {}
    rz = {}

    def down(n, g):
        def tile(i, carry):
            c0 = pl.multiple_of(i * 256, 256)
            val = dot(mid[g], wdf[:, pl.ds(pl.multiple_of(n * cw + i * 256, 256), 256)])
            yout[n, g, :, pl.ds(c0, 256)] = val.astype(BF16)
            return carry

        lax.fori_loop(0, cw // 256, tile, 0)
        for j in range(1, NP):
            t = lax.rem(p + j, NP)
            ry[n, g, j] = remote(
                yout.at[n, g, pl.ds(t * seg, seg), :],
                ans.at[n, g, pl.ds(p * seg, seg), :],
                ry_s.at[n, g, j],
                ry_r.at[n, g, j],
                plane(j),
            )
        mine = pltpu.make_async_copy(
            yout.at[n, g, pl.ds(p * seg, seg), :],
            ans.at[n, g, pl.ds(p * seg, seg), :],
            ry_s.at[n, g, 0],
        )
        mine.start()
        ry[n, g, 0] = mine

    def combine(n, g):
        for j in range(1, NP):
            ry[n, g, j].wait_recv()
        ry[n, g, 0].wait()
        part = dot(wcomb[g, 0], ans[n, g]) + dot(wcomb[g, 1], ans[n, g])
        psnd[n, pl.ds(g * per * n_rows, per * n_rows), :] = part.astype(BF16)
        for i in range(g * per, (g + 1) * per):
            off = order[i]
            if off == 0:
                continue
            slot = pos[nz - off]
            rz[n, slot] = remote(
                psnd.at[n, pl.ds(i * n_rows, n_rows), :],
                prcv.at[n, pl.ds(slot * n_rows, n_rows), :],
                rz_s.at[n, i],
                rz_r.at[n, slot],
                line(off),
            )

    def gather_home(n):
        total = psnd[n, 0:n_rows, :].astype(F32)
        for slot in range(1, nz):
            rz[n, slot].wait_recv()
            total = total + prcv[n, slot * n_rows : (slot + 1) * n_rows, :].astype(F32)
        cols = slice(n * cw, (n + 1) * cw)
        comb[:, cols] = hid_ref[:, cols] + total

    local[2].wait()
    for n in range(CHUNKS):
        for side in range(2):
            wd_c[n, side, 1 - side].wait_recv()
            wd_f[n, side].wait_recv()
        for g in range(groups):
            down(n, g)
        if n >= 1:
            for g in range(groups):
                combine(n - 1, g)
        if n >= 2:
            gather_home(n - 2)
    for g in range(groups):
        combine(CHUNKS - 1, g)
    gather_home(CHUNKS - 2)
    gather_home(CHUNKS - 1)
    out_ref[...] = normalize(comb[...], gain_ref[...]).astype(BF16)
    for c in sends:
        c.wait_send()


def moe(x, hidden, ids, shares, w_gate, w_up, w_down, gain):
    nd = lax.axis_size("dp")
    experts = lax.axis_size("expert")
    nz = experts // NP
    order = [0]
    for k in range(1, nz // 2 + 1):
        order.append(k)
        if nz - k != k:
            order.append(nz - k)
    n_rows, width = x.shape
    kd, ff = w_gate.shape
    kf = w_down.shape[0]
    cw = width // CHUNKS
    per = nz // 2
    seg = per * CAP
    gsz = NP * seg
    vmem = pl.BlockSpec(memory_space=pltpu.VMEM)
    hbm = pl.BlockSpec(memory_space=pl.ANY)
    dma = pltpu.SemaphoreType.DMA
    return pl.pallas_call(
        functools.partial(moe_kernel, (nd, nz, order)),
        out_shape=jax.ShapeDtypeStruct((n_rows, width), BF16),
        in_specs=[vmem, vmem, vmem, vmem, hbm, hbm, hbm, vmem],
        out_specs=vmem,
        scratch_shapes=[
            pltpu.VMEM((nd * kd, ff), BF16),
            pltpu.VMEM((nd * kd, ff), BF16),
            pltpu.VMEM((nd * kf, width), BF16),
            pltpu.VMEM((nz * n_rows, width), BF16),
            pltpu.VMEM((nz, 2 * NP, 128), F32),
            pltpu.VMEM((nz, 2 * NP, 128), F32),
            pltpu.VMEM((2, gsz, width), BF16),
            pltpu.VMEM((2, gsz, width), BF16),
            pltpu.VMEM((2, gsz, ff), BF16),
            pltpu.VMEM((CHUNKS, 2, gsz, cw), BF16),
            pltpu.VMEM((CHUNKS, 2, gsz, cw), BF16),
            pltpu.VMEM((2, 2, per * n_rows, gsz), BF16),
            pltpu.VMEM((CHUNKS, nz * n_rows, cw), BF16),
            pltpu.VMEM((CHUNKS, nz * n_rows, cw), BF16),
            pltpu.VMEM((n_rows, width), F32),
            dma((4,)),
            dma((2, 2, 3)),
            dma((2, 2, 3)),
            dma((CHUNKS, 2, 3)),
            dma((CHUNKS, 2, 3)),
            dma((2, nz)),
            dma((2, nz)),
            dma((2, NP)),
            dma((2, NP)),
            dma((CHUNKS, 2, NP)),
            dma((CHUNKS, 2, NP)),
            dma((CHUNKS, nz)),
            dma((CHUNKS, nz)),
        ],
        compiler_params=pltpu.CompilerParams(
            collective_id=0, has_side_effects=True, vmem_limit_bytes=60 << 20
        ),
    )(x, hidden, ids, shares, w_gate, w_up, w_down, gain)


def shards(
    queries,
    kv_pool,
    page_table,
    ctx_lens,
    w_out,
    residual,
    moe_gain,
    expert_ids,
    route_weights,
    w_gate,
    w_up,
    w_down,
    final_gain,
):
    scale = 1.0 / math.sqrt(HD)
    group_rows = queries.shape[0]
    local_feats = queries.shape[1]
    local_heads = local_feats // HD
    seq_count = page_table.shape[0]
    seq_rows = group_rows // seq_count
    pool_here = kv_pool.shape[1]
    local_pages = page_table - lax.axis_index("expert") * pool_here
    keys = kv_pool[0][local_pages].reshape(seq_count, CTX, local_heads, HD)
    values = kv_pool[1][local_pages].reshape(seq_count, CTX, local_heads, HD)
    asked = queries.reshape(seq_count, seq_rows, local_heads, HD)
    scores = jnp.einsum("sqhd,skhd->shqk", asked, keys, preferred_element_type=F32) * scale
    lengths = ctx_lens.reshape(seq_count, seq_rows)
    visible = (jnp.arange(CTX, dtype=jnp.int32)[None, None, :] < lengths[:, :, None])[:, None]
    scores = jnp.where(visible, scores, -1e30)
    top_score = jnp.max(scores, axis=-1, keepdims=True)
    expo = jnp.where(visible, jnp.exp(scores - top_score), 0.0)
    probs = (expo / jnp.sum(expo, axis=-1, keepdims=True)).astype(BF16)
    mixed = jnp.einsum("shqk,skhd->sqhd", probs, values, preferred_element_type=F32)
    context = mixed.astype(BF16).reshape(group_rows, local_feats)
    columns = lax.all_gather(w_out, "expert", axis=1, tiled=True)
    projected = lax.psum_scatter(
        jnp.dot(context, columns, preferred_element_type=F32).astype(BF16),
        "dp",
        scatter_dimension=0,
        tiled=True,
    ).astype(F32)
    hidden_state = residual.astype(F32) + projected
    moe_input = normalize(hidden_state, moe_gain).astype(BF16)
    rows_here = moe_input.shape[0]
    ids = jnp.full((8, 128), -1, jnp.int32).at[:TOP, :rows_here].set(expert_ids.T)
    shares = jnp.zeros((8, 128), F32).at[:TOP, :rows_here].set(route_weights.T)
    return moe(
        moe_input, hidden_state, ids, shares, w_gate[0], w_up[0], w_down[0], final_gain[None, :]
    )


def solution(mesh):
    return jax.shard_map(
        shards,
        mesh=mesh,
        in_specs=(
            P("expert", "dp"),
            P(None, "expert", None, "dp"),
            P("expert", None),
            P("expert"),
            P("dp", "expert"),
            P(("expert", "dp"), None),
            P(),
            P(("expert", "dp"), None),
            P(("expert", "dp"), None),
            P("expert", "dp", None),
            P("expert", "dp", None),
            P("expert", "dp", None),
            P(),
        ),
        out_specs=P(("expert", "dp"), None),
        check_vma=False,
    )
```

time: 471 us -> 336 us (0.71)
  Pallas kernels: 0 us -> 206 us
  waiting for transfers between devices: 263 us -> 98.3 us
  blocking collectives: 107 us -> 0 us
  matrix products: 35.4 us -> 4.47 us
  local copies, waits for them, and re-layouts: 31.1 us -> 8.59 us
  starting transfers between devices: 11.2 us -> 0.04 us
    pallas_call x0 -> x1, Pallas kernels: none -> 206 us  [moe(): pl.pallas_call(functools.partial(moe_kernel, (nd, nz, order)), out_shape=...]
    all_to_all x1 -> x0, blocking collectives: 107 us -> none  [shards(): lax.all_to_all(outbound, 'expert', split_axis=0, concat_axis=0, tiled=True)]
    all_to_all x1 -> x0, waiting for transfers between devices: 94 us -> none  [shards(): lax.all_to_all(done, 'expert', split_axis=0, concat_axis=0, tiled=True)]
    all_gather x3 -> x0, waiting for transfers between devices: 73 us -> none  [the longest x1 66.3 us: fetch_experts(): lax.all_gather(w_gate, 'dp', axis=1, tiled=True)]
    dot_general x5 -> x2, matrix products: 33.8 us -> 3.76 us  [the longest x1 3.37 us: shards(): jnp.dot(context, columns, preferred_element_type=F32).astype(BF16)]
    reshape x4 -> x0, local copies, waits for them, and re-layouts: 18.2 us -> none  [the longest x1 6.07 us: shards(): done = done.reshape(arrived.shape[0], arrived.shape[1], arrived.shape[2])]
    all_to_all x1 -> x0, starting transfers between devices: 11.1 us -> none  [shards(): lax.all_to_all(done, 'expert', split_axis=0, concat_axis=0, tiled=True)]
    reduce_sum x4 -> x0, other arithmetic: 5.2 us -> none  [the longest x1 3.74 us: shards(): jnp.sum(route_weights[:, :, None] * answers.astype(jnp.float32), axis=1)]
  transfers between devices with their start and end apart: 6 -> 2, of which waited for: 5 -> 2; matrix products, arithmetic and copies ran while one was open for 7% -> 3% of each run, Pallas kernels for 0% -> 0%
where the time goes in v1:
time: 336 us; the launch traced here: 335 us
  Pallas kernels  206 us (61%)
  waiting for transfers between devices  98.3 us (29%)
  between operations  13.5 us (4%)
  local copies, waits for them, and re-layouts  8.59 us (3%)
  other arithmetic  4.49 us (1%)
  matrix products  4.47 us (1%)
    pallas_call x1, Pallas kernels, moe(): pl.pallas_call(functools.partial(moe_kernel, (nd, nz, order)), out_shape=...  206 us
    all_gather x1, waiting for transfers between devices, shards(): columns = lax.all_gather(w_out, 'expert', axis=1, tiled=True)  76.7 us
    reduce_scatter x1, waiting for transfers between devices, shards(): lax.psum_scatter(jnp.dot(context, columns, preferred_element_type=F32).as...  20.9 us
  transfers between devices with their start and end apart: 2, of which 2 were waited for; matrix products, arithmetic and copies ran while one was open for 3% of the time, Pallas kernels for 0%

profile of v1, /device:TPU:1, one launch (start us, length us, event | category | flops | bytes accessed | tf_op | source)
XLA Modules:
  0.0 335.0 jit_solution(8942600330487043016)
XLA Ops:
  6.5 0.7 all-gather.2.cloned.1.call-update
  7.3 0.7 compare_select_fusion
  8.0 0.1 reshape.90
  8.1 1.7 slice_bitcast_fusion
  9.8 0.6 gather_fusion.1
  10.4 1.1 reshape.85
  11.6 0.8 reshape.86
  12.3 0.1 lt.25
  12.4 0.6 gather_fusion
  13.0 0.3 reshape.84
  13.3 0.1 iota_compare_fusion
  13.4 0.2 copy-done
  13.7 0.7 fusion.13
  14.4 0.4 fusion.6
  14.8 0.2 copy.20
  15.0 76.7 %all-gather.2.cloned.1.call-done = bf16[512,2048]{0,1:T(8,128)(2,1)} async-done(((bf16[512,32]{0,1:T(8,128)(2,1)}), bf16[512,2048]{0,1:T(8,128)(2,1)}) %all-gather.2.cloned.1.call-update) | async-done | bytes 2097168 | tf_op jit(solution)/shard_map/all_gather | solution.py:442
  91.7 3.4 %convolution_convert_fusion = bf16[256,2048]{1,0:T(8,128)(2,1)} fusion(bf16[512,2048]{0,1:T(8,128)(2,1)} %all-gather.2.cloned.1.call-done, bf16[32,8,4,128]{3,2,1,0:T(4,128)(2,1)S(1)} %bitcast.27), kind=kOutput, calls=%fused_computation.3 | convolution fusion | flops 537395200 | bytes 3407872 | tf_op jit(solution)/shard_map/dot_general | solution.py:444
  95.1 0.6 scatter.6.ids_ref
  95.7 0.6 scatter.9.rw_ref
  96.3 20.9 %reduce-scatter.2.cloned.1.call-done = bf16[64,2048]{1,0:T(8,128)(2,1)} async-done(((bf16[256,2048]{1,0:T(8,128)(2,1)}), bf16[64,2048]{1,0:T(8,128)(2,1)}) %reduce-scatter.2.cloned.1.call-update) | async-done | bytes 262160 | tf_op jit(solution)/shard_map/reduce_scatter | solution.py:443
  117.2 1.9 convert_add_fusion
  119.1 1.8 multiply_convert_fusion.x_ref
  120.9 205.6 %shard_map.127 = bf16[64,2048]{1,0:T(8,128)(2,1)} custom-call(bf16[64,2048]{1,0:T(8,128)(2,1)} %multiply_convert_fusion.x_ref, f32[64,2048]{1,0:T(8,128)} %get-tuple-element.31.hid_ref, s32[8,128]{1,0:T(8,128)} %scatter.6.ids_ref, f32[8,128]{1,0:T(8,128)} %scatter.9.rw_ref, bf16[512,1408]{1,0:T(8,128)(2,1)} %bitcast.24, bf16[512,1408]{1,0:T(8,128)(2,1)} %bitcast.25, ...), custom_call_target="tpu_custom_call" | custom-call | tf_op jit(solution)/shard_map/pallas_call | solution.py:366
  326.5 1.7 copy.37
  (20 shorter events, 0.1 us)
Async XLA Ops:
  6.5 85.1 %all-gather.2.cloned.1.call-start = ((), (), s32[]{:S(2)}) async-start(), calls=%async_computation.1 | async-start | bytes 2129920 | tf_op jit(solution)/shard_map/all_gather | solution.py:442
  7.3 109.9 %reduce-scatter.2.cloned.1.call-start = ((), (), s32[]{:S(2)}) async-start(), calls=%async_computation.2 | async-start | bytes 1310720 | tf_op jit(solution)/shard_map/reduce_scatter | solution.py:443
  9.8 1.8 copy-start.2
  9.8 2.5 copy-start.7
  12.4 1.2 copy-start
  12.4 1.3 copy-start.3
  91.7 3.4 %copy-start.5 = (s32[64,6]{0,1:T(8,128)S(1)}, s32[64,6]{0,1:T(8,128)}, u32[]{:S(2)}) copy-start(s32[64,6]{0,1:T(8,128)} %param.24) | copy-start | bytes 4612
  91.7 4.0 %copy-start.6 = (f32[64,6]{0,1:T(8,128)S(1)}, f32[64,6]{0,1:T(8,128)}, u32[]{:S(2)}) copy-start(f32[64,6]{0,1:T(8,128)} %param.25) | copy-start | bytes 4612
  91.7 25.5 %copy-start.1 = (bf16[64,2048]{1,0:T(8,128)(2,1)S(1)}, bf16[64,2048]{1,0:T(8,128)(2,1)}, u32[]{:S(2)}) copy-start(bf16[64,2048]{1,0:T(8,128)(2,1)} %param.22) | copy-start | bytes 786436
  91.7 27.4 %copy-start.4 = (f32[2048]{0:T(1024)S(1)}, f32[2048]{0:T(1024)}, u32[]{:S(2)}) copy-start(f32[2048]{0:T(1024)} %param.23) | copy-start | bytes 24580
Sparse Core Ops, SparseCore 0:
  10.1 81.5 all-gather.1
  95.2 21.9 reduce-scatter.1

commit v2 on v1

--- a/solution.py
+++ b/solution.py
@@ -10,7 +10,6 @@
 
 HD = 128
 TOP = 6
-CTX = 256
 CAP = 12
 NP = 8
 CHUNKS = 4
@@ -34,8 +33,13 @@
 
 def moe_kernel(
     sizes,
-    x_ref,
-    hid_ref,
+    table_ref,
+    q_ref,
+    kv_ref,
+    lens_ref,
+    wot_ref,
+    res_ref,
+    mgain_ref,
     ids_ref,
     rw_ref,
     wg_ref,
@@ -43,6 +47,14 @@
     wd_ref,
     gain_ref,
     out_ref,
+    kvs,
+    keys,
+    vals,
+    ctx,
+    wo,
+    prs,
+    prr,
+    hid,
     wgf,
     wuf,
     wdf,
@@ -59,6 +71,14 @@
     prcv,
     comb,
     loc_sem,
+    w1_s,
+    w1_r,
+    w2_s,
+    w2_r,
+    w3_s,
+    w3_r,
+    pr_s,
+    pr_r,
     gu_s,
     gu_r,
     wd_s,
@@ -80,7 +100,7 @@
     e = lax.axis_index("expert")
     z = e // NP
     p = lax.rem(e, NP)
-    n_rows, width = x_ref.shape
+    n_rows, width = res_ref.shape
     kd = wg_ref.shape[0]
     ff = wg_ref.shape[1]
     kf = wd_ref.shape[0]
@@ -97,6 +117,9 @@
     def line(off):
         return (d, lax.rem(z + off, nz) * NP + p)
 
+    def across(k):
+        return (lax.rem(d + k, nd), e)
+
     def remote(src, dst, s, r, to):
         c = pltpu.make_async_remote_copy(
             src_ref=src, dst_ref=dst, send_sem=s, recv_sem=r, device_id=to, device_id_type=MESH
@@ -105,51 +128,26 @@
         sends.append(c)
         return c
 
+    kv_c = pltpu.make_async_copy(kv_ref, kvs, loc_sem.at[4])
+    kv_c.start()
     barrier = pltpu.get_barrier_semaphore()
-    peers = [(right, e), (left, e)] + [line(o) for o in range(1, nz)] + [plane(j) for j in range(1, NP)]
+    peers = [across(k) for k in range(1, nd)]
+    peers += [line(o) for o in range(1, nz)] + [plane(j) for j in range(1, NP)]
     for peer in peers:
         pl.semaphore_signal(barrier, inc=1, device_id=peer, device_id_type=MESH)
+    wo[z, p] = wot_ref[...]
     pl.semaphore_wait(barrier, len(peers))
 
-    rows[pl.ds(0, n_rows), :] = x_ref[...]
-    lanes = ids_ref.shape[1]
-    experts = nz * NP
-    named = jnp.zeros((experts, lanes), F32)
-    share = jnp.zeros((experts, lanes), F32)
-    for k in range(TOP):
-        hit = ids_ref[k : k + 1, :] == iota((experts, lanes), 0)
-        named = named + jnp.where(hit, 1.0, 0.0)
-        share = share + jnp.where(hit, rw_ref[k : k + 1, :], 0.0)
-    upper = jnp.where(iota((lanes, lanes), 0) < iota((lanes, lanes), 1), 1.0, 0.0).astype(BF16)
-    rank = dot(named.astype(BF16), upper)
-    rank = jnp.where(named > 0.5, rank, -1.0)
-    for i in range(nz):
-        route_out[i, 0:NP, :] = rank[i * NP : (i + 1) * NP, :]
-        route_out[i, NP : 2 * NP, :] = share[i * NP : (i + 1) * NP, :]
-    own_route = pltpu.make_async_copy(route_out.at[z], route.at[0], loc_sem.at[3])
-    own_route.start()
-    za = {}
+    w1 = {}
     for off in order[1:]:
-        slot = pos[nz - off]
-        zt = lax.rem(z + off, nz)
-        a = remote(route_out.at[zt], route.at[slot], za_s.at[0, off], za_r.at[0, slot], line(off))
-        b = remote(
-            x_ref, rows.at[pl.ds(slot * n_rows, n_rows), :], za_s.at[1, off], za_r.at[1, slot], line(off)
-        )
-        za[slot] = (a, b)
+        w1[off] = remote(wot_ref, wo.at[z, p], w1_s.at[off], w1_r.at[off], line(off))
 
     gu = [(wg_ref, wgf), (wu_ref, wuf)]
     half = kd // 2
-    local = []
-    for m, (src, dst) in enumerate(gu):
-        c = pltpu.make_async_copy(src, dst.at[pl.ds(d * kd, kd), :], loc_sem.at[m])
-        c.start()
-        local.append(c)
-    c = pltpu.make_async_copy(wd_ref, wdf.at[pl.ds(d * kf, kf), :], loc_sem.at[2])
-    c.start()
-    local.append(c)
     gu_c = {}
-    for m, (src, dst) in enumerate(gu):
+
+    def ring_start(m):
+        src, dst = gu[m]
         for side, to in ((0, right), (1, left)):
             for h in (side, 1 - side):
                 gu_c[m, side, h] = remote(
@@ -160,6 +158,125 @@
                     (to, e),
                 )
 
+    ring_start(0)
+
+    experts = nz * NP
+    lanes = 128
+    named = jnp.zeros((n_rows, lanes), F32)
+    share = jnp.zeros((n_rows, lanes), F32)
+    for k in range(TOP):
+        hit = ids_ref[:, k : k + 1] == iota((n_rows, lanes), 1)
+        named = named + jnp.where(hit, 1.0, 0.0)
+        share = share + jnp.where(hit, rw_ref[:, k : k + 1], 0.0)
+    named = jnp.transpose(named)
+    share = jnp.transpose(share)
+    upper = jnp.where(iota((n_rows, n_rows), 0) < iota((n_rows, n_rows), 1), 1.0, 0.0).astype(BF16)
+    rank = dot(named.astype(BF16), upper)
+    rank = jnp.where(named > 0.5, rank, -1.0)
+    for i in range(nz):
+        route_out[i, 0:NP, :] = rank[i * NP : (i + 1) * NP, :]
+        route_out[i, NP : 2 * NP, :] = share[i * NP : (i + 1) * NP, :]
+    own_route = pltpu.make_async_copy(route_out.at[z], route.at[0], loc_sem.at[3])
+    own_route.start()
+    zr = {}
+    for off in order[1:]:
+        slot = pos[nz - off]
+        zt = lax.rem(z + off, nz)
+        zr[slot] = remote(
+            route_out.at[zt], route.at[slot], za_s.at[0, off], za_r.at[0, slot], line(off)
+        )
+
+    for off in order[1:]:
+        w1[off].wait_recv()
+    sib = p + 1 - 2 * lax.rem(p, 2)
+    sib_to = (d, z * NP + sib)
+    w2 = {}
+    w3 = {}
+    for k in range(1, NP // 2):
+        w2[k] = remote(wo.at[:, p], wo.at[:, p], w2_s.at[k], w2_r.at[k], plane(2 * k))
+    w3[0] = remote(wo.at[:, p], wo.at[:, p], w3_s.at[0], w3_r.at[0], sib_to)
+
+    seqs = table_ref.shape[0]
+    pages = table_ref.shape[1]
+    pool = kv_ref.shape[1]
+    page = kv_ref.shape[2]
+    span = pages * page
+    q_rows = q_ref.shape[0] // seqs
+    scale = 1.0 / math.sqrt(HD)
+    kv_c.wait()
+
+    def attend(s, carry):
+        for i in range(pages):
+            at = lax.rem(table_ref[s, i], pool)
+            keys[i * page : (i + 1) * page, :] = kvs[0, at]
+            vals[i * page : (i + 1) * page, :] = kvs[1, at]
+        here = pl.ds(pl.multiple_of(s * q_rows, q_rows), q_rows)
+        seen = iota((q_rows, span), 1) < lens_ref[here, :]
+        for h in range(q_ref.shape[1] // HD):
+            cols = slice(h * HD, (h + 1) * HD)
+            sc = lax.dot_general(
+                q_ref[here, cols], keys[:, cols], (((1,), (1,)), ((), ())), preferred_element_type=F32
+            )
+            sc = jnp.where(seen, sc * scale, -1e30)
+            ex = jnp.where(seen, jnp.exp(sc - jnp.max(sc, axis=-1, keepdims=True)), 0.0)
+            pr = (ex / jnp.sum(ex, axis=-1, keepdims=True)).astype(BF16)
+            ctx[here, cols] = dot(pr, vals[:, cols]).astype(BF16)
+        return carry
+
+    lax.fori_loop(0, seqs, attend, 0)
+
+    for k in range(1, NP // 2):
+        w2[k].wait_recv()
+        got = lax.rem(p + NP - 2 * k, NP)
+        w3[k] = remote(wo.at[:, got], wo.at[:, got], w3_s.at[k], w3_r.at[k], sib_to)
+    for k in range(NP // 2):
+        w3[k].wait_recv()
+
+    wn = NP * wot_ref.shape[0]
+
+    def project(i, carry):
+        w = wo[i].reshape(wn, wot_ref.shape[1])
+        val = lax.dot_general(
+            ctx[...], w, (((1,), (1,)), ((), ())), preferred_element_type=F32
+        ).astype(BF16)
+        cols = pl.ds(pl.multiple_of(i * wn, wn), wn)
+        for j in range(nd):
+            prs[j, :, cols] = val[j * n_rows : (j + 1) * n_rows, :]
+        return carry
+
+    lax.fori_loop(0, nz, project, 0)
+    pr = {}
+    for k in (2, 1, 3):
+        pr[k] = remote(
+            prs.at[lax.rem(d + k, nd)], prr.at[k], pr_s.at[k], pr_r.at[k], across(k)
+        )
+    ring_start(1)
+    local = []
+    for m, (src, dst) in enumerate(gu):
+        c = pltpu.make_async_copy(src, dst.at[pl.ds(d * kd, kd), :], loc_sem.at[m])
+        c.start()
+        local.append(c)
+    c = pltpu.make_async_copy(wd_ref, wdf.at[pl.ds(d * kf, kf), :], loc_sem.at[2])
+    c.start()
+    local.append(c)
+    state = res_ref[...].astype(F32) + prs[d].astype(F32)
+    for k in (1, 3, 2):
+        pr[k].wait_recv()
+        state = state + prr[k].astype(F32)
+    hid[...] = state
+    rows[pl.ds(0, n_rows), :] = normalize(state, mgain_ref[...]).astype(BF16)
+
+    za = {}
+    for off in order[1:]:
+        slot = pos[nz - off]
+        za[slot] = remote(
+            rows.at[pl.ds(0, n_rows), :],
+            rows.at[pl.ds(slot * n_rows, n_rows), :],
+            za_s.at[1, off],
+            za_r.at[1, slot],
+            line(off),
+        )
+
     slot_i = iota((gsz, per * n_rows), 0)
     expand = jnp.where(iota((gsz, NP), 0) // seg == iota((gsz, NP), 1), 1.0, 0.0).astype(BF16)
     want = lax.rem(slot_i, CAP).astype(F32)
@@ -171,8 +288,8 @@
             if i == 0:
                 own_route.wait()
             else:
-                za[i][0].wait_recv()
-                za[i][1].wait_recv()
+                zr[i].wait_recv()
+                za[i].wait_recv()
         ranks = jnp.concatenate(
             [route[i, 0:NP, 0:n_rows] for i in range(g * per, (g + 1) * per)], axis=1
         )
@@ -321,7 +438,7 @@
             rz[n, slot].wait_recv()
             total = total + prcv[n, slot * n_rows : (slot + 1) * n_rows, :].astype(F32)
         cols = slice(n * cw, (n + 1) * cw)
-        comb[:, cols] = hid_ref[:, cols] + total
+        comb[:, cols] = hid[:, cols] + total
 
     local[2].wait()
     for n in range(CHUNKS):
@@ -344,66 +461,6 @@
         c.wait_send()
 
 
-def moe(x, hidden, ids, shares, w_gate, w_up, w_down, gain):
-    nd = lax.axis_size("dp")
-    experts = lax.axis_size("expert")
-    nz = experts // NP
-    order = [0]
-    for k in range(1, nz // 2 + 1):
-        order.append(k)
-        if nz - k != k:
-            order.append(nz - k)
-    n_rows, width = x.shape
-    kd, ff = w_gate.shape
-    kf = w_down.shape[0]
-    cw = width // CHUNKS
-    per = nz // 2
-    seg = per * CAP
-    gsz = NP * seg
-    vmem = pl.BlockSpec(memory_space=pltpu.VMEM)
-    hbm = pl.BlockSpec(memory_space=pl.ANY)
-    dma = pltpu.SemaphoreType.DMA
-    return pl.pallas_call(
-        functools.partial(moe_kernel, (nd, nz, order)),
-        out_shape=jax.ShapeDtypeStruct((n_rows, width), BF16),
-        in_specs=[vmem, vmem, vmem, vmem, hbm, hbm, hbm, vmem],
-        out_specs=vmem,
-        scratch_shapes=[
-            pltpu.VMEM((nd * kd, ff), BF16),
-            pltpu.VMEM((nd * kd, ff), BF16),
-            pltpu.VMEM((nd * kf, width), BF16),
-            pltpu.VMEM((nz * n_rows, width), BF16),
-            pltpu.VMEM((nz, 2 * NP, 128), F32),
-            pltpu.VMEM((nz, 2 * NP, 128), F32),
-            pltpu.VMEM((2, gsz, width), BF16),
-            pltpu.VMEM((2, gsz, width), BF16),
-            pltpu.VMEM((2, gsz, ff), BF16),
-            pltpu.VMEM((CHUNKS, 2, gsz, cw), BF16),
-            pltpu.VMEM((CHUNKS, 2, gsz, cw), BF16),
-            pltpu.VMEM((2, 2, per * n_rows, gsz), BF16),
-            pltpu.VMEM((CHUNKS, nz * n_rows, cw), BF16),
-            pltpu.VMEM((CHUNKS, nz * n_rows, cw), BF16),
-            pltpu.VMEM((n_rows, width), F32),
-            dma((4,)),
-            dma((2, 2, 3)),
-            dma((2, 2, 3)),
-            dma((CHUNKS, 2, 3)),
-            dma((CHUNKS, 2, 3)),
-            dma((2, nz)),
-            dma((2, nz)),
-            dma((2, NP)),
-            dma((2, NP)),
-            dma((CHUNKS, 2, NP)),
-            dma((CHUNKS, 2, NP)),
-            dma((CHUNKS, nz)),
-            dma((CHUNKS, nz)),
-        ],
-        compiler_params=pltpu.CompilerParams(
-            collective_id=0, has_side_effects=True, vmem_limit_bytes=60 << 20
-        ),
-    )(x, hidden, ids, shares, w_gate, w_up, w_down, gain)
-
-
 def shards(
     queries,
     kv_pool,
@@ -419,40 +476,97 @@
     w_down,
     final_gain,
 ):
-    scale = 1.0 / math.sqrt(HD)
-    group_rows = queries.shape[0]
-    local_feats = queries.shape[1]
-    local_heads = local_feats // HD
-    seq_count = page_table.shape[0]
-    seq_rows = group_rows // seq_count
-    pool_here = kv_pool.shape[1]
-    local_pages = page_table - lax.axis_index("expert") * pool_here
-    keys = kv_pool[0][local_pages].reshape(seq_count, CTX, local_heads, HD)
-    values = kv_pool[1][local_pages].reshape(seq_count, CTX, local_heads, HD)
-    asked = queries.reshape(seq_count, seq_rows, local_heads, HD)
-    scores = jnp.einsum("sqhd,skhd->shqk", asked, keys, preferred_element_type=F32) * scale
-    lengths = ctx_lens.reshape(seq_count, seq_rows)
-    visible = (jnp.arange(CTX, dtype=jnp.int32)[None, None, :] < lengths[:, :, None])[:, None]
-    scores = jnp.where(visible, scores, -1e30)
-    top_score = jnp.max(scores, axis=-1, keepdims=True)
-    expo = jnp.where(visible, jnp.exp(scores - top_score), 0.0)
-    probs = (expo / jnp.sum(expo, axis=-1, keepdims=True)).astype(BF16)
-    mixed = jnp.einsum("shqk,skhd->sqhd", probs, values, preferred_element_type=F32)
-    context = mixed.astype(BF16).reshape(group_rows, local_feats)
-    columns = lax.all_gather(w_out, "expert", axis=1, tiled=True)
-    projected = lax.psum_scatter(
-        jnp.dot(context, columns, preferred_element_type=F32).astype(BF16),
-        "dp",
-        scatter_dimension=0,
-        tiled=True,
-    ).astype(F32)
-    hidden_state = residual.astype(F32) + projected
-    moe_input = normalize(hidden_state, moe_gain).astype(BF16)
-    rows_here = moe_input.shape[0]
-    ids = jnp.full((8, 128), -1, jnp.int32).at[:TOP, :rows_here].set(expert_ids.T)
-    shares = jnp.zeros((8, 128), F32).at[:TOP, :rows_here].set(route_weights.T)
-    return moe(
-        moe_input, hidden_state, ids, shares, w_gate[0], w_up[0], w_down[0], final_gain[None, :]
+    nd = lax.axis_size("dp")
+    experts = lax.axis_size("expert")
+    nz = experts // NP
+    order = [0]
+    for k in range(1, nz // 2 + 1):
+        order.append(k)
+        if nz - k != k:
+            order.append(nz - k)
+    n_rows, width = residual.shape
+    group_rows, feats = queries.shape
+    _, pool, page, _ = kv_pool.shape
+    span = page_table.shape[1] * page
+    wc = w_out.shape[1]
+    kd, ff = w_gate.shape[1:]
+    kf = w_down.shape[1]
+    cw = width // CHUNKS
+    per = nz // 2
+    seg = per * CAP
+    gsz = NP * seg
+    vmem = pl.BlockSpec(memory_space=pltpu.VMEM)
+    smem = pl.BlockSpec(memory_space=pltpu.SMEM)
+    hbm = pl.BlockSpec(memory_space=pl.ANY)
+    dma = pltpu.SemaphoreType.DMA
+    return pl.pallas_call(
+        functools.partial(moe_kernel, (nd, nz, order)),
+        out_shape=jax.ShapeDtypeStruct((n_rows, width), BF16),
+        in_specs=[smem, vmem, hbm, vmem, vmem, vmem, vmem, vmem, vmem, hbm, hbm, hbm, vmem],
+        out_specs=vmem,
+        scratch_shapes=[
+            pltpu.VMEM((2, pool, page, feats), BF16),
+            pltpu.VMEM((span, feats), BF16),
+            pltpu.VMEM((span, feats), BF16),
+            pltpu.VMEM((group_rows, feats), BF16),
+            pltpu.VMEM((nz, NP, wc, feats), BF16),
+            pltpu.VMEM((nd, n_rows, width), BF16),
+            pltpu.VMEM((nd, n_rows, width), BF16),
+            pltpu.VMEM((n_rows, width), F32),
+            pltpu.VMEM((nd * kd, ff), BF16),
+            pltpu.VMEM((nd * kd, ff), BF16),
+            pltpu.VMEM((nd * kf, width), BF16),
+            pltpu.VMEM((nz * n_rows, width), BF16),
+            pltpu.VMEM((nz, 2 * NP, n_rows), F32),
+            pltpu.VMEM((nz, 2 * NP, n_rows), F32),
+            pltpu.VMEM((2, gsz, width), BF16),
+            pltpu.VMEM((2, gsz, width), BF16),
+            pltpu.VMEM((2, gsz, ff), BF16),
+            pltpu.VMEM((CHUNKS, 2, gsz, cw), BF16),
+            pltpu.VMEM((CHUNKS, 2, gsz, cw), BF16),
+            pltpu.VMEM((2, 2, per * n_rows, gsz), BF16),
+            pltpu.VMEM((CHUNKS, nz * n_rows, cw), BF16),
+            pltpu.VMEM((CHUNKS, nz * n_rows, cw), BF16),
+            pltpu.VMEM((n_rows, width), F32),
+            dma((5,)),
+            dma((nz,)),
+            dma((nz,)),
+            dma((NP // 2,)),
+            dma((NP // 2,)),
+            dma((NP // 2,)),
+            dma((NP // 2,)),
+            dma((nd,)),
+            dma((nd,)),
+            dma((2, 2, 3)),
+            dma((2, 2, 3)),
+            dma((CHUNKS, 2, 3)),
+            dma((CHUNKS, 2, 3)),
+            dma((2, nz)),
+            dma((2, nz)),
+            dma((2, NP)),
+            dma((2, NP)),
+            dma((CHUNKS, 2, NP)),
+            dma((CHUNKS, 2, NP)),
+            dma((CHUNKS, nz)),
+            dma((CHUNKS, nz)),
+        ],
+        compiler_params=pltpu.CompilerParams(
+            collective_id=0, has_side_effects=True, vmem_limit_bytes=62 << 20
+        ),
+    )(
+        page_table,
+        queries,
+        kv_pool,
+        ctx_lens[:, None],
+        w_out.T,
+        residual,
+        moe_gain[None, :],
+        expert_ids,
+        route_weights,
+        w_gate[0],
+        w_up[0],
+        w_down[0],
+        final_gain[None, :],
     )
 
 

time: 336 us -> 244 us (0.73)
  waiting for transfers between devices: 98.3 us -> 0 us
  Pallas kernels: 206 us -> 237 us
  between operations: 13.5 us -> 0.01 us
  other arithmetic: 4.49 us -> 0 us
  matrix products: 4.47 us -> 0 us
    all_gather x1 -> x0, waiting for transfers between devices: 76.7 us -> none  [shards(): columns = lax.all_gather(w_out, 'expert', axis=1, tiled=True)]
    pallas_call x1, Pallas kernels: 206 us -> 237 us  [shards(): pl.pallas_call(functools.partial(moe_kernel, (nd, nz, order)), out_shape=...]
    reduce_scatter x1 -> x0, waiting for transfers between devices: 20.9 us -> none  [shards(): lax.psum_scatter(jnp.dot(context, columns, preferred_element_type=F32).as...]
    dot_general x2 -> x0, matrix products: 3.76 us -> none  [the longest x1 3.37 us: shards(): jnp.dot(context, columns, preferred_element_type=F32).astype(BF16)]
  transfers between devices with their start and end apart: 2 -> 0, of which waited for: 2 -> 0; matrix products, arithmetic and copies ran while one was open for 3% -> 0% of each run, Pallas kernels for 0% -> 0%
where the time goes in v2:
time: 244 us; the launch traced here: 243 us
  Pallas kernels  237 us (97%)
  local copies, waits for them, and re-layouts  5.89 us (2%)
    pallas_call x1, Pallas kernels, shards(): pl.pallas_call(functools.partial(moe_kernel, (nd, nz, order)), out_shape=...  237 us

profile of v2, /device:TPU:1, one launch (start us, length us, event | category | flops | bytes accessed | tf_op | source)
XLA Modules:
  0.0 242.6 jit_solution(11778179031096932122)
XLA Ops:
  0.0 1.4 copy.17.ids_ref
  1.4 1.4 copy.18.rw_ref
  2.8 1.5 copy.16.lens_ref
  4.2 236.7 %shard_map.127 = bf16[64,2048]{1,0:T(8,128)(2,1)} custom-call(s32[4,4]{1,0:T(4,128)} %table_ref.1, bf16[256,512]{1,0:T(8,128)(2,1)} %q_ref.1, bf16[2,16,64,512]{3,2,1,0:T(8,128)(2,1)} %kv_ref.1, s32[256,1]{1,0:T(8,128)} %copy.16.lens_ref, bf16[32,512]{1,0:T(8,128)(2,1)} %bitcast.10, bf16[64,2048]{1,0:T(8,128)(2,1)} %res_ref.1, f32[1,2048]{1,0:T(1,128)} %bitcast.11, ...), custom_call_target="tpu_custom_call" | custom-call | tf_op jit(solution)/shard_map/pallas_call | solution.py:502
  240.9 1.7 copy.20

commit v3 on v2

--- a/solution.py
+++ b/solution.py
@@ -48,6 +48,7 @@
     gain_ref,
     out_ref,
     kvs,
+    lens_t,
     keys,
     vals,
     ctx,
@@ -66,6 +67,7 @@
     mid,
     yout,
     ans,
+    picks,
     wcomb,
     psnd,
     prcv,
@@ -161,15 +163,12 @@
     ring_start(0)
 
     experts = nz * NP
-    lanes = 128
-    named = jnp.zeros((n_rows, lanes), F32)
-    share = jnp.zeros((n_rows, lanes), F32)
+    named = jnp.zeros((experts, n_rows), F32)
+    share = jnp.zeros((experts, n_rows), F32)
     for k in range(TOP):
-        hit = ids_ref[:, k : k + 1] == iota((n_rows, lanes), 1)
+        hit = ids_ref[k : k + 1, :] == iota((experts, n_rows), 0)
         named = named + jnp.where(hit, 1.0, 0.0)
-        share = share + jnp.where(hit, rw_ref[:, k : k + 1], 0.0)
-    named = jnp.transpose(named)
-    share = jnp.transpose(share)
+        share = share + jnp.where(hit, rw_ref[k : k + 1, :], 0.0)
     upper = jnp.where(iota((n_rows, n_rows), 0) < iota((n_rows, n_rows), 1), 1.0, 0.0).astype(BF16)
     rank = dot(named.astype(BF16), upper)
     rank = jnp.where(named > 0.5, rank, -1.0)
@@ -203,6 +202,7 @@
     span = pages * page
     q_rows = q_ref.shape[0] // seqs
     scale = 1.0 / math.sqrt(HD)
+    lens_t[...] = jnp.transpose(jnp.broadcast_to(lens_ref[...], (128, lens_ref.shape[1])))
     kv_c.wait()
 
     def attend(s, carry):
@@ -211,7 +211,7 @@
             keys[i * page : (i + 1) * page, :] = kvs[0, at]
             vals[i * page : (i + 1) * page, :] = kvs[1, at]
         here = pl.ds(pl.multiple_of(s * q_rows, q_rows), q_rows)
-        seen = iota((q_rows, span), 1) < lens_ref[here, :]
+        seen = iota((q_rows, span), 1) < lens_t[here, 0:1]
         for h in range(q_ref.shape[1] // HD):
             cols = slice(h * HD, (h + 1) * HD)
             sc = lax.dot_general(
@@ -259,6 +259,28 @@
     c = pltpu.make_async_copy(wd_ref, wdf.at[pl.ds(d * kf, kf), :], loc_sem.at[2])
     c.start()
     local.append(c)
+
+    slot_i = iota((gsz, per * n_rows), 0)
+    expand = jnp.where(iota((gsz, NP), 0) // seg == iota((gsz, NP), 1), 1.0, 0.0).astype(BF16)
+    want = lax.rem(slot_i, CAP).astype(F32)
+    block_ok = lax.rem(slot_i, seg) // CAP == iota((gsz, per * n_rows), 1) // n_rows
+    for g in range(groups):
+        members = range(g * per, (g + 1) * per)
+        for i in members:
+            if i == 0:
+                own_route.wait()
+            else:
+                zr[i].wait_recv()
+        ranks = jnp.concatenate([route[i, 0:NP, :] for i in members], axis=1)
+        shares = jnp.concatenate([route[i, NP : 2 * NP, :] for i in members], axis=1)
+        pick = jnp.logical_and(dot(expand, ranks.astype(BF16)) == want, block_ok)
+        picks[g] = jnp.where(pick, 1.0, 0.0).astype(BF16)
+        hi = shares.astype(BF16)
+        lo = (shares - hi.astype(F32)).astype(BF16)
+        for part, val in ((0, hi), (1, lo)):
+            full = jnp.where(pick, dot(expand, val), 0.0)
+            wcomb[g, part] = jnp.transpose(full).astype(BF16)
+
     state = res_ref[...].astype(F32) + prs[d].astype(F32)
     for k in (1, 3, 2):
         pr[k].wait_recv()
@@ -266,47 +288,84 @@
     hid[...] = state
     rows[pl.ds(0, n_rows), :] = normalize(state, mgain_ref[...]).astype(BF16)
 
+    far = nz // 2
+    hr = n_rows // 2
     za = {}
-    for off in order[1:]:
-        slot = pos[nz - off]
-        za[slot] = remote(
-            rows.at[pl.ds(0, n_rows), :],
-            rows.at[pl.ds(slot * n_rows, n_rows), :],
-            za_s.at[1, off],
-            za_r.at[1, slot],
-            line(off),
+
+    def hop(side, k):
+        off_here = ((nz - (k - 1)) if side == 0 else (k - 1)) % nz
+        off_there = (nz - k) if side == 0 else k
+        src0 = pos[off_here] * n_rows
+        dst0 = pos[off_there] * n_rows
+        size = n_rows
+        if k == far:
+            size = hr
+            src0 += side * hr
+            dst0 += side * hr
+        za[side, k] = remote(
+            rows.at[pl.ds(src0, size), :],
+            rows.at[pl.ds(dst0, size), :],
+            za_s.at[1 + side, k],
+            za_r.at[1 + side, k],
+            line(1 if side == 0 else nz - 1),
         )
 
-    slot_i = iota((gsz, per * n_rows), 0)
-    expand = jnp.where(iota((gsz, NP), 0) // seg == iota((gsz, NP), 1), 1.0, 0.0).astype(BF16)
-    want = lax.rem(slot_i, CAP).astype(F32)
-    block_ok = lax.rem(slot_i, seg) // CAP == iota((gsz, per * n_rows), 1) // n_rows
+    def relay(k):
+        for side in range(2):
+            za[side, k].wait_recv()
+            if k < far:
+                hop(side, k + 1)
+
+    for side in range(2):
+        hop(side, 1)
+
+    hf = kf // 2
+    gu_f = {}
+    wd_c = {}
+    wd_f = {}
+
+    def gu_forward(m):
+        dst = gu[m][1]
+        for side, frm, to in ((0, left, right), (1, right, left)):
+            gu_c[m, side, side].wait_recv()
+            at = pl.ds(frm * kd + side * half, half)
+            gu_f[m, side] = remote(
+                dst.at[at, :], dst.at[at, :], gu_s.at[m, side, 2], gu_r.at[m, side, 2], (to, e)
+            )
+
+    def wd_start(n):
+        cols = pl.ds(n * cw, cw)
+        for side, to in ((0, right), (1, left)):
+            for h in (side, 1 - side):
+                wd_c[n, side, h] = remote(
+                    wd_ref.at[pl.ds(h * hf, hf), cols],
+                    wdf.at[pl.ds(d * kf + h * hf, hf), cols],
+                    wd_s.at[n, side, h],
+                    wd_r.at[n, side, h],
+                    (to, e),
+                )
+
+    def wd_forward(n):
+        cols = pl.ds(n * cw, cw)
+        for side, frm, to in ((0, left, right), (1, right, left)):
+            wd_c[n, side, side].wait_recv()
+            at = pl.ds(frm * kf + side * hf, hf)
+            wd_f[n, side] = remote(
+                wdf.at[at, cols], wdf.at[at, cols], wd_s.at[n, side, 2], wd_r.at[n, side, 2], (to, e)
+            )
+
     ya = {}
 
     def dispatch(g):
-        for i in range(g * per, (g + 1) * per):
-            if i == 0:
-                own_route.wait()
-            else:
-                zr[i].wait_recv()
-                za[i].wait_recv()
-        ranks = jnp.concatenate(
-            [route[i, 0:NP, 0:n_rows] for i in range(g * per, (g + 1) * per)], axis=1
-        )
-        shares = jnp.concatenate(
-            [route[i, NP : 2 * NP, 0:n_rows] for i in range(g * per, (g + 1) * per)], axis=1
-        )
-        pick = jnp.logical_and(dot(expand, ranks.astype(BF16)) == want, block_ok)
-        pick_b = jnp.where(pick, 1.0, 0.0).astype(BF16)
         base = g * per * n_rows
 
         def tile(i, carry):
             cols = pl.ds(pl.multiple_of(i * 512, 512), 512)
-            snd[g, :, cols] = dot(pick_b, rows[pl.ds(base, per * n_rows), cols]).astype(BF16)
+            snd[g, :, cols] = dot(picks[g], rows[pl.ds(base, per * n_rows), cols]).astype(BF16)
             return carry
 
         lax.fori_loop(0, width // 512, tile, 0)
-        for j in range(1, NP):
+        for j in (4, 5, 3, 2, 6, 7, 1):
             t = lax.rem(p + j, NP)
             ya[g, j] = remote(
                 snd.at[g, pl.ds(t * seg, seg), :],
@@ -320,50 +379,22 @@
         )
         mine.start()
         ya[g, 0] = mine
-        hi = shares.astype(BF16)
-        lo = (shares - hi.astype(F32)).astype(BF16)
-        for part, val in ((0, hi), (1, lo)):
-            full = jnp.where(pick, dot(expand, val), 0.0)
-            wcomb[g, part] = jnp.transpose(full).astype(BF16)
-
-    for g in range(groups):
-        dispatch(g)
-
-    gu_f = {}
-    for m, (_, dst) in enumerate(gu):
-        for side, frm, to in ((0, left, right), (1, right, left)):
-            gu_c[m, side, side].wait_recv()
-            at = pl.ds(frm * kd + side * half, half)
-            gu_f[m, side] = remote(
-                dst.at[at, :], dst.at[at, :], gu_s.at[m, side, 2], gu_r.at[m, side, 2], (to, e)
-            )
-    hf = kf // 2
-    wd_c = {}
-    for n in range(CHUNKS):
-        cols = pl.ds(n * cw, cw)
-        for side, to in ((0, right), (1, left)):
-            for h in (side, 1 - side):
-                wd_c[n, side, h] = remote(
-                    wd_ref.at[pl.ds(h * hf, hf), cols],
-                    wdf.at[pl.ds(d * kf + h * hf, hf), cols],
-                    wd_s.at[n, side, h],
-                    wd_r.at[n, side, h],
-                    (to, e),
-                )
+
+    gu_forward(0)
+    for k in range(1, far // 2 + 1):
+        relay(k)
+    dispatch(0)
+    for k in range(far // 2 + 1, far + 1):
+        relay(k)
+    dispatch(1)
+    gu_forward(1)
+    wd_start(0)
+    wd_start(1)
     for m in range(2):
         local[m].wait()
         for side in range(2):
             gu_c[m, side, 1 - side].wait_recv()
             gu_f[m, side].wait_recv()
-    wd_f = {}
-    for n in range(CHUNKS):
-        cols = pl.ds(n * cw, cw)
-        for side, frm, to in ((0, left, right), (1, right, left)):
-            wd_c[n, side, side].wait_recv()
-            at = pl.ds(frm * kf + side * hf, hf)
-            wd_f[n, side] = remote(
-                wdf.at[at, cols], wdf.at[at, cols], wd_s.at[n, side, 2], wd_r.at[n, side, 2], (to, e)
-            )
 
     def up_tile(g, cols):
         xs = xin[g]
@@ -384,6 +415,8 @@
         lax.fori_loop(0, full_tiles, step, 0)
         if ff % 256:
             up_tile(g, pl.ds(full_tiles * 256, ff % 256))
+        wd_forward(g)
+        wd_start(g + 2)
 
     ry = {}
     rz = {}
@@ -447,6 +480,8 @@
             wd_f[n, side].wait_recv()
         for g in range(groups):
             down(n, g)
+        if n + 2 < CHUNKS:
+            wd_forward(n + 2)
         if n >= 1:
             for g in range(groups):
                 combine(n - 1, g)
@@ -506,6 +541,7 @@
         out_specs=vmem,
         scratch_shapes=[
             pltpu.VMEM((2, pool, page, feats), BF16),
+            pltpu.VMEM((group_rows, 128), jnp.int32),
             pltpu.VMEM((span, feats), BF16),
             pltpu.VMEM((span, feats), BF16),
             pltpu.VMEM((group_rows, feats), BF16),
@@ -524,6 +560,7 @@
             pltpu.VMEM((2, gsz, ff), BF16),
             pltpu.VMEM((CHUNKS, 2, gsz, cw), BF16),
             pltpu.VMEM((CHUNKS, 2, gsz, cw), BF16),
+            pltpu.VMEM((2, gsz, per * n_rows), BF16),
             pltpu.VMEM((2, 2, per * n_rows, gsz), BF16),
             pltpu.VMEM((CHUNKS, nz * n_rows, cw), BF16),
             pltpu.VMEM((CHUNKS, nz * n_rows, cw), BF16),
@@ -541,8 +578,8 @@
             dma((2, 2, 3)),
             dma((CHUNKS, 2, 3)),
             dma((CHUNKS, 2, 3)),
-            dma((2, nz)),
-            dma((2, nz)),
+            dma((3, nz)),
+            dma((3, nz)),
             dma((2, NP)),
             dma((2, NP)),
             dma((CHUNKS, 2, NP)),
@@ -557,12 +594,12 @@
         page_table,
         queries,
         kv_pool,
-        ctx_lens[:, None],
+        ctx_lens[None, :],
         w_out.T,
         residual,
         moe_gain[None, :],
-        expert_ids,
-        route_weights,
+        expert_ids.T,
+        route_weights.T,
         w_gate[0],
         w_up[0],
         w_down[0],

time: 244 us -> 206 us (0.84)
  Pallas kernels: 237 us -> 203 us
  local copies, waits for them, and re-layouts: 5.89 us -> 1.67 us
    pallas_call x1, Pallas kernels: 237 us -> 203 us  [shards(): pl.pallas_call(functools.partial(moe_kernel, (nd, nz, order)), out_shape=...]
    unnamed x3 -> x1, local copies, waits for them, and re-layouts: 4.42 us -> 1.67 us
where the time goes in v3:
time: 206 us; the launch traced here: 205 us
  Pallas kernels  203 us (99%)
    pallas_call x1, Pallas kernels, shards(): pl.pallas_call(functools.partial(moe_kernel, (nd, nz, order)), out_shape=...  203 us

profile of v3, /device:TPU:1, one launch (start us, length us, event | category | flops | bytes accessed | tf_op | source)
XLA Modules:
  0.0 204.9 jit_solution(1638432679282008662)
XLA Ops:
  0.0 203.2 %shard_map.127 = bf16[64,2048]{1,0:T(8,128)(2,1)} custom-call(s32[4,4]{1,0:T(4,128)} %table_ref.1, bf16[256,512]{1,0:T(8,128)(2,1)} %q_ref.1, bf16[2,16,64,512]{3,2,1,0:T(8,128)(2,1)} %kv_ref.1, s32[1,256]{1,0:T(1,128)} %bitcast.17, bf16[32,512]{1,0:T(8,128)(2,1)} %bitcast.12, bf16[64,2048]{1,0:T(8,128)(2,1)} %res_ref.1, f32[1,2048]{1,0:T(1,128)} %bitcast.13, ...), custom_call_target="tpu_custom_call" | custom-call | tf_op jit(solution)/shard_map/pallas_call | solution.py:537
  203.2 1.7 copy.15

commit v4 on v3

--- a/solution.py
+++ b/solution.py
@@ -12,7 +12,9 @@
 TOP = 6
 CAP = 12
 NP = 8
-CHUNKS = 4
+WIDTHS = (256, 384, 384, 384, 256, 256, 128)
+STARTS = (0, 256, 640, 1024, 1408, 1664, 1920)
+CHUNKS = 7
 MESH = pl.DeviceIdType.MESH
 F32 = jnp.float32
 BF16 = jnp.bfloat16
@@ -106,7 +108,6 @@
     kd = wg_ref.shape[0]
     ff = wg_ref.shape[1]
     kf = wd_ref.shape[0]
-    cw = width // CHUNKS
     seg = per * CAP
     gsz = NP * seg
     right = lax.rem(d + 1, nd)
@@ -148,19 +149,23 @@
     half = kd // 2
     gu_c = {}
 
-    def ring_start(m):
+    parts = ((0, 512), (512, 512), (1024, ff - 1024))
+    cut = 6 * 128
+
+    def ring_start(m, goes_on, i=0, c0=0, cn=ff):
         src, dst = gu[m]
         for side, to in ((0, right), (1, left)):
-            for h in (side, 1 - side):
-                gu_c[m, side, h] = remote(
-                    src.at[pl.ds(h * half, half), :],
-                    dst.at[pl.ds(d * kd + h * half, half), :],
-                    gu_s.at[m, side, h],
-                    gu_r.at[m, side, h],
-                    (to, e),
-                )
-
-    ring_start(0)
+            h = side if goes_on else 1 - side
+            gu_c[m, side, h, i] = remote(
+                src.at[pl.ds(h * half, half), pl.ds(c0, cn)],
+                dst.at[pl.ds(d * kd + h * half, half), pl.ds(c0, cn)],
+                gu_s.at[m, side, h + i],
+                gu_r.at[m, side, h + i],
+                (to, e),
+            )
+
+    ring_start(0, True)
+    ring_start(0, False, 0, 0, cut)
 
     experts = nz * NP
     named = jnp.zeros((experts, n_rows), F32)
@@ -250,7 +255,9 @@
         pr[k] = remote(
             prs.at[lax.rem(d + k, nd)], prr.at[k], pr_s.at[k], pr_r.at[k], across(k)
         )
-    ring_start(1)
+    ring_start(0, False, 2, cut, ff - cut)
+    ring_start(1, True)
+    ring_start(1, False)
     local = []
     for m, (src, dst) in enumerate(gu):
         c = pltpu.make_async_copy(src, dst.at[pl.ds(d * kd, kd), :], loc_sem.at[m])
@@ -324,35 +331,50 @@
     wd_c = {}
     wd_f = {}
 
-    def gu_forward(m):
-        dst = gu[m][1]
-        for side, frm, to in ((0, left, right), (1, right, left)):
-            gu_c[m, side, side].wait_recv()
-            at = pl.ds(frm * kd + side * half, half)
-            gu_f[m, side] = remote(
-                dst.at[at, :], dst.at[at, :], gu_s.at[m, side, 2], gu_r.at[m, side, 2], (to, e)
+    def gu_forward():
+        for m in range(2):
+            for side in range(2):
+                gu_c[m, side, side, 0].wait_recv()
+        for i, (c0, cn) in enumerate(parts):
+            for m in range(2):
+                dst = gu[m][1]
+                for side, frm, to in ((0, left, right), (1, right, left)):
+                    at = pl.ds(frm * kd + side * half, half)
+                    gu_f[m, side, i] = remote(
+                        dst.at[at, pl.ds(c0, cn)],
+                        dst.at[at, pl.ds(c0, cn)],
+                        gu_s.at[m, side, 4 + i],
+                        gu_r.at[m, side, 4 + i],
+                        (to, e),
+                    )
+
+    def wd_start(n, goes_on):
+        cols = pl.ds(STARTS[n], WIDTHS[n])
+        for side, to in ((0, right), (1, left)):
+            h = side if goes_on else 1 - side
+            wd_c[n, side, h] = remote(
+                wd_ref.at[pl.ds(h * hf, hf), cols],
+                wdf.at[pl.ds(d * kf + h * hf, hf), cols],
+                wd_s.at[n, side, h],
+                wd_r.at[n, side, h],
+                (to, e),
             )
 
-    def wd_start(n):
-        cols = pl.ds(n * cw, cw)
-        for side, to in ((0, right), (1, left)):
-            for h in (side, 1 - side):
-                wd_c[n, side, h] = remote(
-                    wd_ref.at[pl.ds(h * hf, hf), cols],
-                    wdf.at[pl.ds(d * kf + h * hf, hf), cols],
-                    wd_s.at[n, side, h],
-                    wd_r.at[n, side, h],
-                    (to, e),
-                )
-
     def wd_forward(n):
-        cols = pl.ds(n * cw, cw)
+        cols = pl.ds(STARTS[n], WIDTHS[n])
         for side, frm, to in ((0, left, right), (1, right, left)):
             wd_c[n, side, side].wait_recv()
             at = pl.ds(frm * kf + side * hf, hf)
             wd_f[n, side] = remote(
                 wdf.at[at, cols], wdf.at[at, cols], wd_s.at[n, side, 2], wd_r.at[n, side, 2], (to, e)
             )
+
+    def wd_next(n):
+        if n < CHUNKS:
+            wd_forward(n)
+            wd_start(n, False)
+        if n + 2 < CHUNKS:
+            wd_start(n + 2, True)
 
     ya = {}
 
@@ -380,21 +402,23 @@
         mine.start()
         ya[g, 0] = mine
 
-    gu_forward(0)
     for k in range(1, far // 2 + 1):
         relay(k)
     dispatch(0)
-    for k in range(far // 2 + 1, far + 1):
+    relay(far // 2 + 1)
+    gu_forward()
+    for k in range(far // 2 + 2, far + 1):
         relay(k)
     dispatch(1)
-    gu_forward(1)
-    wd_start(0)
-    wd_start(1)
+    wd_start(0, True)
+    wd_start(1, True)
     for m in range(2):
         local[m].wait()
+    for side in range(2):
+        gu_c[0, side, 1 - side, 2].wait_recv()
+    for m in range(2):
         for side in range(2):
-            gu_c[m, side, 1 - side].wait_recv()
-            gu_f[m, side].wait_recv()
+            gu_c[m, side, 1 - side, 0].wait_recv()
 
     def up_tile(g, cols):
         xs = xin[g]
@@ -402,93 +426,97 @@
         up = dot(xs, wuf[:, cols])
         mid[g, :, cols] = (gate / (1.0 + jnp.exp(-gate)) * up).astype(BF16)
 
-    full_tiles = ff // 256
-    for g in range(groups):
-        for j in range(1, NP):
-            ya[g, j].wait_recv()
-        ya[g, 0].wait()
-
-        def step(i, carry, g=g):
-            up_tile(g, pl.ds(pl.multiple_of(i * 256, 256), 256))
-            return carry
-
-        lax.fori_loop(0, full_tiles, step, 0)
-        if ff % 256:
-            up_tile(g, pl.ds(full_tiles * 256, ff % 256))
-        wd_forward(g)
-        wd_start(g + 2)
+    for i, (c0, cn) in enumerate(parts):
+        for m in range(2):
+            for side in range(2):
+                gu_f[m, side, i].wait_recv()
+        for g in range(groups):
+            if i == 0:
+                for j in range(1, NP):
+                    ya[g, j].wait_recv()
+                ya[g, 0].wait()
+
+            def step(t, carry, g=g, c0=c0):
+                up_tile(g, pl.ds(pl.multiple_of(c0 + t * 256, 256), 256))
+                return carry
+
+            lax.fori_loop(0, cn // 256, step, 0)
+            if cn % 256:
+                up_tile(g, pl.ds(c0 + cn // 256 * 256, cn % 256))
 
     ry = {}
     rz = {}
 
-    def down(n, g):
-        def tile(i, carry):
-            c0 = pl.multiple_of(i * 256, 256)
-            val = dot(mid[g], wdf[:, pl.ds(pl.multiple_of(n * cw + i * 256, 256), 256)])
-            yout[n, g, :, pl.ds(c0, 256)] = val.astype(BF16)
-            return carry
-
-        lax.fori_loop(0, cw // 256, tile, 0)
-        for j in range(1, NP):
+    def down(n):
+        def tile(g, c0, cn):
+            cols = pl.ds(c0, cn)
+            yout[g, :, cols] = dot(mid[g], wdf[:, cols]).astype(BF16)
+
+        for g in range(groups):
+            for c in range(0, WIDTHS[n], 256):
+                tile(g, STARTS[n] + c, min(256, WIDTHS[n] - c))
+        cols = pl.ds(STARTS[n], WIDTHS[n])
+        for j in (4, 5, 3, 2, 6, 7, 1):
             t = lax.rem(p + j, NP)
-            ry[n, g, j] = remote(
-                yout.at[n, g, pl.ds(t * seg, seg), :],
-                ans.at[n, g, pl.ds(p * seg, seg), :],
-                ry_s.at[n, g, j],
-                ry_r.at[n, g, j],
+            ry[n, j] = remote(
+                yout.at[:, pl.ds(t * seg, seg), cols],
+                ans.at[:, pl.ds(p * seg, seg), cols],
+                ry_s.at[n, j],
+                ry_r.at[n, j],
                 plane(j),
             )
         mine = pltpu.make_async_copy(
-            yout.at[n, g, pl.ds(p * seg, seg), :],
-            ans.at[n, g, pl.ds(p * seg, seg), :],
-            ry_s.at[n, g, 0],
+            yout.at[:, pl.ds(p * seg, seg), cols],
+            ans.at[:, pl.ds(p * seg, seg), cols],
+            ry_s.at[n, 0],
         )
         mine.start()
-        ry[n, g, 0] = mine
-
-    def combine(n, g):
+        ry[n, 0] = mine
+
+    def combine(n):
+        cols = pl.ds(STARTS[n], WIDTHS[n])
         for j in range(1, NP):
-            ry[n, g, j].wait_recv()
-        ry[n, g, 0].wait()
-        part = dot(wcomb[g, 0], ans[n, g]) + dot(wcomb[g, 1], ans[n, g])
-        psnd[n, pl.ds(g * per * n_rows, per * n_rows), :] = part.astype(BF16)
-        for i in range(g * per, (g + 1) * per):
-            off = order[i]
-            if off == 0:
-                continue
-            slot = pos[nz - off]
-            rz[n, slot] = remote(
-                psnd.at[n, pl.ds(i * n_rows, n_rows), :],
-                prcv.at[n, pl.ds(slot * n_rows, n_rows), :],
-                rz_s.at[n, i],
-                rz_r.at[n, slot],
-                line(off),
-            )
+            ry[n, j].wait_recv()
+        ry[n, 0].wait()
+        for g in (1, 0):
+            part = dot(wcomb[g, 0], ans[g, :, cols]) + dot(wcomb[g, 1], ans[g, :, cols])
+            psnd[g * per * n_rows : (g + 1) * per * n_rows, cols] = part.astype(BF16)
+            for i in range((g + 1) * per - 1, g * per - 1, -1):
+                off = order[i]
+                if off == 0:
+                    continue
+                slot = pos[nz - off]
+                rz[n, slot] = remote(
+                    psnd.at[pl.ds(i * n_rows, n_rows), cols],
+                    prcv.at[pl.ds(slot * n_rows, n_rows), cols],
+                    rz_s.at[n, i],
+                    rz_r.at[n, slot],
+                    line(off),
+                )
 
     def gather_home(n):
-        total = psnd[n, 0:n_rows, :].astype(F32)
+        cols = slice(STARTS[n], STARTS[n] + WIDTHS[n])
+        total = psnd[0:n_rows, cols].astype(F32)
         for slot in range(1, nz):
             rz[n, slot].wait_recv()
-            total = total + prcv[n, slot * n_rows : (slot + 1) * n_rows, :].astype(F32)
-        cols = slice(n * cw, (n + 1) * cw)
+            total = total + prcv[slot * n_rows : (slot + 1) * n_rows, cols].astype(F32)
         comb[:, cols] = hid[:, cols] + total
 
+    wd_next(0)
+    wd_next(1)
     local[2].wait()
     for n in range(CHUNKS):
         for side in range(2):
             wd_c[n, side, 1 - side].wait_recv()
             wd_f[n, side].wait_recv()
-        for g in range(groups):
-            down(n, g)
-        if n + 2 < CHUNKS:
-            wd_forward(n + 2)
+        down(n)
         if n >= 1:
-            for g in range(groups):
-                combine(n - 1, g)
-        if n >= 2:
-            gather_home(n - 2)
-    for g in range(groups):
-        combine(CHUNKS - 1, g)
+            combine(n - 1)
+        wd_next(n + 2)
+        if n >= 3:
+            gather_home(n - 3)
+    combine(CHUNKS - 1)
+    gather_home(CHUNKS - 3)
     gather_home(CHUNKS - 2)
     gather_home(CHUNKS - 1)
     out_ref[...] = normalize(comb[...], gain_ref[...]).astype(BF16)
@@ -526,7 +554,6 @@
     wc = w_out.shape[1]
     kd, ff = w_gate.shape[1:]
     kf = w_down.shape[1]
-    cw = width // CHUNKS
     per = nz // 2
     seg = per * CAP
     gsz = NP * seg
@@ -558,12 +585,12 @@
             pltpu.VMEM((2, gsz, width), BF16),
             pltpu.VMEM((2, gsz, width), BF16),
             pltpu.VMEM((2, gsz, ff), BF16),
-            pltpu.VMEM((CHUNKS, 2, gsz, cw), BF16),
-            pltpu.VMEM((CHUNKS, 2, gsz, cw), BF16),
+            pltpu.VMEM((2, gsz, width), BF16),
+            pltpu.VMEM((2, gsz, width), BF16),
             pltpu.VMEM((2, gsz, per * n_rows), BF16),
             pltpu.VMEM((2, 2, per * n_rows, gsz), BF16),
-            pltpu.VMEM((CHUNKS, nz * n_rows, cw), BF16),
-            pltpu.VMEM((CHUNKS, nz * n_rows, cw), BF16),
+            pltpu.VMEM((nz * n_rows, width), BF16),
+            pltpu.VMEM((nz * n_rows, width), BF16),
             pltpu.VMEM((n_rows, width), F32),
             dma((5,)),
             dma((nz,)),
@@ -574,16 +601,16 @@
             dma((NP // 2,)),
             dma((nd,)),
             dma((nd,)),
-            dma((2, 2, 3)),
-            dma((2, 2, 3)),
+            dma((2, 2, 7)),
+            dma((2, 2, 7)),
             dma((CHUNKS, 2, 3)),
             dma((CHUNKS, 2, 3)),
             dma((3, nz)),
             dma((3, nz)),
             dma((2, NP)),
             dma((2, NP)),
-            dma((CHUNKS, 2, NP)),
-            dma((CHUNKS, 2, NP)),
+            dma((CHUNKS, NP)),
+            dma((CHUNKS, NP)),
             dma((CHUNKS, nz)),
             dma((CHUNKS, nz)),
         ],

time: 206 us -> 195 us (0.947)
  Pallas kernels: 203 us -> 194 us
    pallas_call x1, Pallas kernels: 203 us -> 194 us  [shards(): pl.pallas_call(functools.partial(moe_kernel, (nd, nz, order)), out_shape=...]
where the time goes in v4:
time: 195 us
  Pallas kernels  194 us (99%)
    pallas_call x1, Pallas kernels, shards(): pl.pallas_call(functools.partial(moe_kernel, (nd, nz, order)), out_shape=...  194 us

profile of v4, /device:TPU:1, one launch (start us, length us, event | category | flops | bytes accessed | tf_op | source)
XLA Modules:
  0.0 195.2 jit_solution(17503832731439891006)
XLA Ops:
  0.0 193.5 %shard_map.127 = bf16[64,2048]{1,0:T(8,128)(2,1)} custom-call(s32[4,4]{1,0:T(4,128)} %table_ref.1, bf16[256,512]{1,0:T(8,128)(2,1)} %q_ref.1, bf16[2,16,64,512]{3,2,1,0:T(8,128)(2,1)} %kv_ref.1, s32[1,256]{1,0:T(1,128)} %bitcast.17, bf16[32,512]{1,0:T(8,128)(2,1)} %bitcast.12, bf16[64,2048]{1,0:T(8,128)(2,1)} %res_ref.1, f32[1,2048]{1,0:T(1,128)} %bitcast.13, ...), custom_call_target="tpu_custom_call" | custom-call | tf_op jit(solution)/shard_map/pallas_call | solution.py:564
  193.5 1.7 copy.15

commit v5 on v4

--- a/solution.py
+++ b/solution.py
@@ -72,7 +72,9 @@
     picks,
     wcomb,
     psnd,
-    prcv,
+    parta,
+    partb,
+    partc,
     comb,
     loc_sem,
     w1_s,
@@ -95,6 +97,8 @@
     ry_r,
     rz_s,
     rz_r,
+    rd_s,
+    rd_r,
 ):
     nd, nz, order = sizes
     pos = {off: i for i, off in enumerate(order)}
@@ -120,9 +124,6 @@
     def line(off):
         return (d, lax.rem(z + off, nz) * NP + p)
 
-    def across(k):
-        return (lax.rem(d + k, nd), e)
-
     def remote(src, dst, s, r, to):
         c = pltpu.make_async_remote_copy(
             src_ref=src, dst_ref=dst, send_sem=s, recv_sem=r, device_id=to, device_id_type=MESH
@@ -134,16 +135,12 @@
     kv_c = pltpu.make_async_copy(kv_ref, kvs, loc_sem.at[4])
     kv_c.start()
     barrier = pltpu.get_barrier_semaphore()
-    peers = [across(k) for k in range(1, nd)]
+    peers = [(right, e), (left, e)]
     peers += [line(o) for o in range(1, nz)] + [plane(j) for j in range(1, NP)]
     for peer in peers:
         pl.semaphore_signal(barrier, inc=1, device_id=peer, device_id_type=MESH)
     wo[z, p] = wot_ref[...]
     pl.semaphore_wait(barrier, len(peers))
-
-    w1 = {}
-    for off in order[1:]:
-        w1[off] = remote(wot_ref, wo.at[z, p], w1_s.at[off], w1_r.at[off], line(off))
 
     gu = [(wg_ref, wgf), (wu_ref, wuf)]
     half = kd // 2
@@ -165,6 +162,10 @@
             )
 
     ring_start(0, True)
+
+    w1 = {}
+    for off in order[1:]:
+        w1[off] = remote(wot_ref, wo.at[z, p], w1_s.at[off], w1_r.at[off], line(off))
     ring_start(0, False, 0, 0, cut)
 
     experts = nz * NP
@@ -251,11 +252,25 @@
 
     lax.fori_loop(0, nz, project, 0)
     pr = {}
-    for k in (2, 1, 3):
-        pr[k] = remote(
-            prs.at[lax.rem(d + k, nd)], prr.at[k], pr_s.at[k], pr_r.at[k], across(k)
+    hw = width // 2
+    opposite = lax.rem(d + 2, nd)
+    for side, to in ((0, right), (1, left)):
+        cols = pl.ds(side * hw, hw)
+        pr[side] = remote(
+            prs.at[opposite, :, cols],
+            prr.at[2, :, cols],
+            pr_s.at[side],
+            pr_r.at[side],
+            (to, e),
         )
     ring_start(0, False, 2, cut, ff - cut)
+    for side, to in ((0, right), (1, left)):
+        pr[side].wait_recv()
+        cols = slice(side * hw, (side + 1) * hw)
+        prs[to, :, cols] = (prs[to, :, cols].astype(F32) + prr[2, :, cols].astype(F32)).astype(BF16)
+        pr[2 + side] = remote(
+            prs.at[to], prr.at[side], pr_s.at[2 + side], pr_r.at[2 + side], (to, e)
+        )
     ring_start(1, True)
     ring_start(1, False)
     local = []
@@ -289,9 +304,9 @@
             wcomb[g, part] = jnp.transpose(full).astype(BF16)
 
     state = res_ref[...].astype(F32) + prs[d].astype(F32)
-    for k in (1, 3, 2):
-        pr[k].wait_recv()
-        state = state + prr[k].astype(F32)
+    for side in range(2):
+        pr[2 + side].wait_recv()
+        state = state + prr[side].astype(F32)
     hid[...] = state
     rows[pl.ds(0, n_rows), :] = normalize(state, mgain_ref[...]).astype(BF16)
 
@@ -446,6 +461,7 @@
 
     ry = {}
     rz = {}
+    rd = {}
 
     def down(n):
         def tile(g, c0, cn):
@@ -481,47 +497,101 @@
         for g in (1, 0):
             part = dot(wcomb[g, 0], ans[g, :, cols]) + dot(wcomb[g, 1], ans[g, :, cols])
             psnd[g * per * n_rows : (g + 1) * per * n_rows, cols] = part.astype(BF16)
-            for i in range((g + 1) * per - 1, g * per - 1, -1):
+        if n == CHUNKS - 1:
+            for i in range(nz - 1, 0, -1):
                 off = order[i]
-                if off == 0:
-                    continue
                 slot = pos[nz - off]
-                rz[n, slot] = remote(
+                rd[slot] = remote(
                     psnd.at[pl.ds(i * n_rows, n_rows), cols],
-                    prcv.at[pl.ds(slot * n_rows, n_rows), cols],
-                    rz_s.at[n, i],
-                    rz_r.at[n, slot],
+                    partc.at[pl.ds(slot * n_rows, n_rows), :],
+                    rd_s.at[i],
+                    rd_r.at[slot],
                     line(off),
+                )
+            return
+        for side in range(2):
+            to = line(2 if side == 0 else nz - 2)
+            near = pos[3 if side == 0 else nz - 3] * n_rows
+            last = pos[far] * n_rows + side * hr
+            for i, (src, dst, size) in enumerate(((last, n_rows, hr), (near, 0, n_rows))):
+                rz[n, side, i] = remote(
+                    psnd.at[pl.ds(src, size), cols],
+                    parta.at[side, pl.ds(dst, size), cols],
+                    rz_s.at[n, side, i],
+                    rz_r.at[n, side, i],
+                    to,
+                )
+
+    def spread(n):
+        cols = pl.ds(STARTS[n], WIDTHS[n])
+        for side in range(2):
+            rz[n, side, 0].wait_recv()
+            rz[n, side, 1].wait_recv()
+            one = pos[1 if side == 0 else nz - 1] * n_rows
+            two = pos[2 if side == 0 else nz - 2] * n_rows
+            for r0, size, got in ((one, n_rows, 0), (two + side * hr, hr, n_rows)):
+                psnd[r0 : r0 + size, cols] = (
+                    psnd[r0 : r0 + size, cols].astype(F32)
+                    + parta[side, got : got + size, cols].astype(F32)
+                ).astype(BF16)
+            for i, (src, dst, steps) in enumerate(((two, n_rows, 2), (one, 0, 1))):
+                rz[n, side, 2 + i] = remote(
+                    psnd.at[pl.ds(src, n_rows), cols],
+                    partb.at[side, pl.ds(dst, n_rows), cols],
+                    rz_s.at[n, side, 2 + i],
+                    rz_r.at[n, side, 2 + i],
+                    line(steps if side == 0 else nz - steps),
                 )
 
     def gather_home(n):
         cols = slice(STARTS[n], STARTS[n] + WIDTHS[n])
         total = psnd[0:n_rows, cols].astype(F32)
-        for slot in range(1, nz):
-            rz[n, slot].wait_recv()
-            total = total + prcv[slot * n_rows : (slot + 1) * n_rows, cols].astype(F32)
+        for slot in range(1, nz if n == CHUNKS - 1 else 0):
+            rd[slot].wait_recv()
+            total = total + partc[slot * n_rows : (slot + 1) * n_rows, :].astype(F32)
+        for side in range(2 if n < CHUNKS - 1 else 0):
+            for i, r0 in ((1, 0), (0, n_rows)):
+                rz[n, side, 2 + i].wait_recv()
+                total = total + partb[side, r0 : r0 + n_rows, cols].astype(F32)
         comb[:, cols] = hid[:, cols] + total
 
     wd_next(0)
     wd_next(1)
     local[2].wait()
+    marks = []
+
+    def drain(count):
+        for c in sends[:count]:
+            if c is not None:
+                c.wait_send()
+        sends[:count] = [None] * count
+
     for n in range(CHUNKS):
+        marks.append(len(sends))
         for side in range(2):
             wd_c[n, side, 1 - side].wait_recv()
             wd_f[n, side].wait_recv()
         down(n)
-        if n >= 1:
+        if n >= 2:
             combine(n - 1)
         wd_next(n + 2)
-        if n >= 3:
-            gather_home(n - 3)
+        if n == 0:
+            combine(0)
+        if n >= 2:
+            spread(n - 2)
+        if n >= 4:
+            gather_home(n - 4)
+        if n >= 1:
+            drain(marks[n - 1])
+    drain(marks[CHUNKS - 1])
     combine(CHUNKS - 1)
+    spread(CHUNKS - 2)
+    gather_home(CHUNKS - 4)
     gather_home(CHUNKS - 3)
     gather_home(CHUNKS - 2)
     gather_home(CHUNKS - 1)
     out_ref[...] = normalize(comb[...], gain_ref[...]).astype(BF16)
-    for c in sends:
-        c.wait_send()
+    drain(len(sends))
 
 
 def shards(
@@ -590,7 +660,9 @@
             pltpu.VMEM((2, gsz, per * n_rows), BF16),
             pltpu.VMEM((2, 2, per * n_rows, gsz), BF16),
             pltpu.VMEM((nz * n_rows, width), BF16),
-            pltpu.VMEM((nz * n_rows, width), BF16),
+            pltpu.VMEM((2, n_rows + n_rows // 2, width), BF16),
+            pltpu.VMEM((2, 2 * n_rows, width), BF16),
+            pltpu.VMEM((nz * n_rows, WIDTHS[-1]), BF16),
             pltpu.VMEM((n_rows, width), F32),
             dma((5,)),
             dma((nz,)),
@@ -611,8 +683,10 @@
             dma((2, NP)),
             dma((CHUNKS, NP)),
             dma((CHUNKS, NP)),
-            dma((CHUNKS, nz)),
-            dma((CHUNKS, nz)),
+            dma((CHUNKS, 2, 4)),
+            dma((CHUNKS, 2, 4)),
+            dma((nz,)),
+            dma((nz,)),
         ],
         compiler_params=pltpu.CompilerParams(
             collective_id=0, has_side_effects=True, vmem_limit_bytes=62 << 20

time: 195 us -> 189 us (0.969)
  Pallas kernels: 194 us -> 188 us
    pallas_call x1, Pallas kernels: 194 us -> 188 us  [shards(): pl.pallas_call(functools.partial(moe_kernel, (nd, nz, order)), out_shape=...]
where the time goes in v5:
time: 189 us
  Pallas kernels  188 us (99%)
    pallas_call x1, Pallas kernels, shards(): pl.pallas_call(functools.partial(moe_kernel, (nd, nz, order)), out_shape=...  188 us

profile of v5, /device:TPU:1, one launch (start us, length us, event | category | flops | bytes accessed | tf_op | source)
XLA Modules:
  0.0 189.2 jit_solution(12891751705396361991)
XLA Ops:
  0.0 187.5 %shard_map.127 = bf16[64,2048]{1,0:T(8,128)(2,1)} custom-call(s32[4,4]{1,0:T(4,128)} %table_ref.1, bf16[256,512]{1,0:T(8,128)(2,1)} %q_ref.1, bf16[2,16,64,512]{3,2,1,0:T(8,128)(2,1)} %kv_ref.1, s32[1,256]{1,0:T(1,128)} %bitcast.17, bf16[32,512]{1,0:T(8,128)(2,1)} %bitcast.12, bf16[64,2048]{1,0:T(8,128)(2,1)} %res_ref.1, f32[1,2048]{1,0:T(1,128)} %bitcast.13, ...), custom_call_target="tpu_custom_call" | custom-call | tf_op jit(solution)/shard_map/pallas_call | solution.py:634
  187.5 1.7 copy.15

commit v6 on v5

--- a/solution.py
+++ b/solution.py
@@ -36,11 +36,11 @@
 def moe_kernel(
     sizes,
     table_ref,
-    q_ref,
+    q_hbm,
     kv_ref,
     lens_ref,
     wot_ref,
-    res_ref,
+    res_hbm,
     mgain_ref,
     ids_ref,
     rw_ref,
@@ -49,6 +49,8 @@
     wd_ref,
     gain_ref,
     out_ref,
+    q_ref,
+    res_ref,
     kvs,
     lens_t,
     keys,
@@ -134,6 +136,10 @@
 
     kv_c = pltpu.make_async_copy(kv_ref, kvs, loc_sem.at[4])
     kv_c.start()
+    q_c = pltpu.make_async_copy(q_hbm, q_ref, loc_sem.at[5])
+    q_c.start()
+    res_c = pltpu.make_async_copy(res_hbm, res_ref, loc_sem.at[6])
+    res_c.start()
     barrier = pltpu.get_barrier_semaphore()
     peers = [(right, e), (left, e)]
     peers += [line(o) for o in range(1, nz)] + [plane(j) for j in range(1, NP)]
@@ -210,6 +216,8 @@
     scale = 1.0 / math.sqrt(HD)
     lens_t[...] = jnp.transpose(jnp.broadcast_to(lens_ref[...], (128, lens_ref.shape[1])))
     kv_c.wait()
+    q_c.wait()
+    res_c.wait()
 
     def attend(s, carry):
         for i in range(pages):
@@ -584,9 +592,9 @@
         if n >= 1:
             drain(marks[n - 1])
     drain(marks[CHUNKS - 1])
+    gather_home(CHUNKS - 4)
     combine(CHUNKS - 1)
     spread(CHUNKS - 2)
-    gather_home(CHUNKS - 4)
     gather_home(CHUNKS - 3)
     gather_home(CHUNKS - 2)
     gather_home(CHUNKS - 1)
@@ -634,9 +642,11 @@
     return pl.pallas_call(
         functools.partial(moe_kernel, (nd, nz, order)),
         out_shape=jax.ShapeDtypeStruct((n_rows, width), BF16),
-        in_specs=[smem, vmem, hbm, vmem, vmem, vmem, vmem, vmem, vmem, hbm, hbm, hbm, vmem],
+        in_specs=[smem, hbm, hbm, vmem, vmem, hbm, vmem, vmem, vmem, hbm, hbm, hbm, vmem],
         out_specs=vmem,
         scratch_shapes=[
+            pltpu.VMEM((group_rows, feats), BF16),
+            pltpu.VMEM((n_rows, width), BF16),
             pltpu.VMEM((2, pool, page, feats), BF16),
             pltpu.VMEM((group_rows, 128), jnp.int32),
             pltpu.VMEM((span, feats), BF16),
@@ -664,7 +674,7 @@
             pltpu.VMEM((2, 2 * n_rows, width), BF16),
             pltpu.VMEM((nz * n_rows, WIDTHS[-1]), BF16),
             pltpu.VMEM((n_rows, width), F32),
-            dma((5,)),
+            dma((7,)),
             dma((nz,)),
             dma((nz,)),
             dma((NP // 2,)),

time: 189 us -> 189 us (level)
  no operation moved by 1% of the time
where the time goes in v6:
time: 189 us
  Pallas kernels  187 us (99%)
    pallas_call x1, Pallas kernels, shards(): pl.pallas_call(functools.partial(moe_kernel, (nd, nz, order)), out_shape=...  187 us

profile of v6, /device:TPU:1, one launch (start us, length us, event | category | flops | bytes accessed | tf_op | source)
XLA Modules:
  0.0 188.7 jit_solution(15812099035986916747)
XLA Ops:
  0.0 187.0 %shard_map.127 = bf16[64,2048]{1,0:T(8,128)(2,1)} custom-call(s32[4,4]{1,0:T(4,128)} %table_ref.1, bf16[256,512]{1,0:T(8,128)(2,1)} %q_hbm.1, bf16[2,16,64,512]{3,2,1,0:T(8,128)(2,1)} %kv_ref.1, s32[1,256]{1,0:T(1,128)} %bitcast.17, bf16[32,512]{1,0:T(8,128)(2,1)} %bitcast.12, bf16[64,2048]{1,0:T(8,128)(2,1)} %res_hbm.1, f32[1,2048]{1,0:T(1,128)} %bitcast.13, ...), custom_call_target="tpu_custom_call" | custom-call | tf_op jit(solution)/shard_map/pallas_call | solution.py:642
  187.0 1.7 copy.15
